TPU v7x, 128 devices: a whole 4x4x4 slice. The times are simulated.
128 devices in a mesh: depth: 4 (over x_lo, core), height: 32 (over x_hi, z, y).
Axes of the slice: x: 4 (x_hi: 2, x_lo: 2; x = x_hi * 2 + x_lo), y: 4, z: 4, core: 2. Of those that a mesh axis runs over, the one named last changes fastest.
Arguments:
- fixed_image: float32 [32, 128, 128], P('depth', 'height'), as said below
- moving_image: float32 [32, 128, 128], P('depth', 'height'), as said below
- conv_one: float32 [64, 1, 3, 3, 3], replicated, may hold values from -1.25 to 1.25
- gain_one: float32 [64], replicated, may hold values from 0.1 to 1.9
- shift_one: float32 [64], replicated, may hold values from -3 to 3
- conv_two: bfloat16 [27, 4096], replicated, may hold values from -0.15625 to 0.15625
- gain_two: float32 [64], replicated, may hold values from 0.1 to 1.9
- shift_two: float32 [64], replicated, may hold values from -3 to 3
- sharpness: float32 [1], replicated, may hold values from 1 to 4
Outputs:
- displacement: float32 [3, 32, 128, 128], P(None, 'depth', 'height')
Inputs may be any that keep to these rules, and one draw needn't show every extreme that they name: `fixed_image`: intensities of a scan; the two scans show the same anatomy. `moving_image`: intensities of a scan; the two scans show the same anatomy.
All inputs are finite; a program needn't handle non-finite values.
Results may differ from a plain program's by a relative error of at most 0.0049.
Values may be sent and summed in bfloat16 or wider, within the bound.
A program may use at most 64 MiB of HBM per device.

v0:
```python
import jax
import jax.numpy as jnp
from jax import lax
from jax.sharding import PartitionSpec as P

RADIUS = 3


def extended(array, sides, width):
    for axis, dim in sides:
        size, length = (lax.axis_size(axis), array.shape[dim])
        up = [(i, (i + 1) % size) for i in range(size - 1)]
        down = [(j, i) for i, j in up]
        last = lax.slice_in_dim(array, length - width, length, axis=dim)
        first = lax.slice_in_dim(array, 0, width, axis=dim)
        before = lax.ppermute(last, axis, up)
        after = lax.ppermute(first, axis, down)
        array = jnp.concatenate([before, array, after], axis=dim)
    return array


def convolve_valid(field, kernel, precise):
    return lax.conv_general_dilated(
        field,
        kernel,
        (1, 1, 1),
        "VALID",
        dimension_numbers=("NCDHW", "OIDHW", "NCDHW"),
        precision=precise,
        preferred_element_type=jnp.float32,
    )


def widen_last(field, amount):
    spec = [(0, 0)] * (field.ndim - 1) + [(amount, amount)]
    return jnp.pad(field, spec)


def normalized(raw, totals, squares, cell_count, gain, shift):
    mean_val = totals / cell_count
    mean_sq = squares / cell_count
    inv_dev = lax.rsqrt(mean_sq - mean_val * mean_val + 1e-05)
    scale_all = (inv_dev * gain[None, :])[:, :, None, None, None]
    offset_all = (shift[None, :] - mean_val * inv_dev * gain[None, :])[:, :, None, None, None]
    return jax.nn.leaky_relu(raw * scale_all + offset_all, 0.01).astype(jnp.bfloat16)


def local(
    fixed_image,
    moving_image,
    conv_one,
    gain_one,
    shift_one,
    conv_two,
    gain_two,
    shift_two,
    sharpness,
):
    slab_cells, strip_cells, width_cells = fixed_image.shape
    channels = gain_one.shape[0]
    cell_count = float(
        slab_cells * strip_cells * width_cells * lax.axis_size("depth") * lax.axis_size("height")
    )
    both_images = jnp.stack([fixed_image, moving_image])
    highest = lax.Precision.HIGHEST
    kernel_second = jnp.transpose(conv_two.reshape(3, 3, 3, channels, channels), (4, 3, 0, 1, 2))
    widened = extended(both_images, (("depth", 1), ("height", 2)), 1)
    widened = widen_last(widened, 1)
    first_raw = convolve_valid(widened[:, None], conv_one, highest)
    totals, squares = lax.psum(
        (jnp.sum(first_raw, axis=(2, 3, 4)), jnp.sum(first_raw * first_raw, axis=(2, 3, 4))),
        ("depth", "height"),
    )
    first_feat = normalized(first_raw, totals, squares, cell_count, gain_one, shift_one)
    first_wide = extended(first_feat, (("depth", 2), ("height", 3)), 1)
    first_wide = widen_last(first_wide, 1)
    second_raw = convolve_valid(first_wide, kernel_second, None)
    totals_two, squares_two = lax.psum(
        (jnp.sum(second_raw, axis=(2, 3, 4)), jnp.sum(second_raw * second_raw, axis=(2, 3, 4))),
        ("depth", "height"),
    )
    features = normalized(second_raw, totals_two, squares_two, cell_count, gain_two, shift_two)
    fixed_wide = features[0].astype(jnp.float32)
    moving_rimmed = extended(features[1], (("depth", 1), ("height", 2)), RADIUS)
    moving_rimmed = widen_last(moving_rimmed, RADIUS)
    factor = sharpness[0] / channels
    span = 2 * RADIUS + 1

    def depth_step(depth_shift, state):
        running_max, running_sum, running_vec = state
        depth_plane = lax.dynamic_slice_in_dim(moving_rimmed, depth_shift, slab_cells, 1)
        depth_offset = (depth_shift - RADIUS).astype(jnp.float32)
        for height_shift in range(span):
            for width_shift in range(span):
                window = depth_plane[
                    :,
                    :,
                    height_shift : height_shift + strip_cells,
                    width_shift : width_shift + width_cells,
                ]
                difference = fixed_wide - window.astype(jnp.float32)
                scores = -factor * jnp.sum(difference * difference, axis=0)
                new_max = jnp.maximum(running_max, scores)
                keep = jnp.exp(running_max - new_max)
                weights = jnp.exp(scores - new_max)
                vector = jnp.stack(
                    [
                        depth_offset,
                        jnp.float32(height_shift - RADIUS),
                        jnp.float32(width_shift - RADIUS),
                    ]
                )
                running_sum = running_sum * keep + weights
                running_vec = running_vec * keep[None] + weights[None] * vector[:, None, None, None]
                running_max = new_max
        return (running_max, running_sum, running_vec)

    cell_shape = (slab_cells, strip_cells, width_cells)
    start = (
        jnp.full(cell_shape, -jnp.inf, jnp.float32),
        jnp.zeros(cell_shape, jnp.float32),
        jnp.zeros((3,) + cell_shape, jnp.float32),
    )
    final = lax.fori_loop(0, span, depth_step, start)
    return final[2] / final[1][None]


def solution(mesh):
    placed = (
        P("depth", "height", None),
        P("depth", "height", None),
        P(),
        P(),
        P(),
        P(),
        P(),
        P(),
        P(),
    )
    return jax.shard_map(
        local,
        mesh=mesh,
        in_specs=placed,
        out_specs=P(None, "depth", "height", None),
        check_vma=False,
    )
```

profile of v0, /device:TPU:1, one launch (start us, length us, event | category | flops | bytes accessed | tf_op | source)
XLA Modules:
  0.0 769.5 jit_solution(13010348486707336937)
XLA Ops:
  0.8 4.5 collective-permute-start
  7.2 3.0 collective-permute-done.1
  11.0 3.2 collective-permute-start.2
  15.5 3.1 collective-permute-done.3
  20.9 18.4 %fusion.39 = (f32[8,4,16,17,64]{4,2,3,1,0:T(8,128)S(1)}, f32[8,4,16,17,64]{4,2,3,1,0:T(8,128)S(1)}) fusion(f32[1,10,6,16,19]{3,0,4,2,1:T(1,128)S(1)} %copy.33, f32[64,1,3,3,3]{0,1,4,3,2:T(1,128)S(1)} %copy-done, pred[16,17]{0,1:T(8,128)(4,1)S(1)} %copy-done.21), kind=kOutput, calls=%fused_computation.385 | convolution fusion | flops 181600256 | bytes 4536592 | tf_op jit(solution)/shard_map/conv_general_dilated | solution.py:23
  39.3 2.6 copy.35
  41.9 2.6 copy.34
  45.0 71.1 %all-reduce.10 = (f32[2,64]{1,0:T(2,128)S(1)}, f32[2,64]{1,0:T(2,128)S(1)}) all-reduce(f32[2,64]{1,0:T(2,128)S(1)} %get-tuple-element.541, f32[2,64]{1,0:T(2,128)S(1)} %get-tuple-element.542), channel_id=1, replica_groups=mesh['depth'=4,'height'=32] {'depth','height'}, use_global_device_ids=true, to_apply=%region_3.4 | all-reduce | flops 256 | bytes 2048 | tf_op jit(solution)/shard_map/psum | solution.py:70
  122.7 3.5 collective-permute-start.4
  127.1 2.3 collective-permute-start.5
  131.3 3.8 collective-permute-done.5
  138.9 2.2 reshape.164
  142.3 3.5 collective-permute-done.7
  147.2 6.1 copy.58
  153.3 6.3 pad.56.clone
  159.9 5.4 fusion.19
  165.3 8.6 %fusion.40 = (f32[8,4,16,17,64]{4,2,3,1,0:T(8,128)S(1)}, f32[8,4,16,17,64]{4,2,3,1,0:T(8,128)S(1)}) fusion(bf16[3,3,3,64,64]{4,3,2,1,0:T(8,128)(2,1)S(1)} %copy-done.15, bf16[64,10,6,2,8,19]{0,3,5,4,2,1:T(2,128)(2,1)S(1)} %fusion.19, pred[16,17]{0,1:T(8,128)(4,1)S(1)} %copy-done.21), kind=kOutput, calls=%fused_computation.386 | convolution fusion | flops 1926299648 | bytes 7012624 | tf_op jit(solution)/shard_map/conv_general_dilated | solution.py:23
  173.9 2.6 copy.47
  177.1 3.0 copy.46
  180.7 72.6 %all-reduce.9 = (f32[2,64]{1,0:T(2,128)S(1)}, f32[2,64]{1,0:T(2,128)S(1)}) all-reduce(f32[2,64]{1,0:T(2,128)S(1)} %slice_reduce_fusion, f32[2,64]{1,0:T(2,128)S(1)} %slice_reduce_fusion.1), channel_id=1, replica_groups=mesh['depth'=4,'height'=32] {'depth','height'}, use_global_device_ids=true, to_apply=%region_7.8 | all-reduce | flops 256 | bytes 2048 | tf_op jit(solution)/shard_map/psum | solution.py:78
  260.5 3.9 collective-permute-start.8
  264.4 1.9 collective-permute-start.9
  267.8 3.0 collective-permute-done.8
  272.1 3.1 collective-permute-done.9
  279.0 2.2 collective-permute-start.10
  284.5 5.9 collective-permute-done.10
  290.4 5.0 collective-permute-done.11
  295.4 6.4 select_maximum_fusion.1
  301.8 466.0 %while.20 = (s32[]{:T(128)}, f32[8,4,128]{2,1,0:T(4,128)}, f32[8,4,128]{2,1,0:T(4,128)}, f32[3,8,4,128]{3,2,1,0:T(4,128)}, f32[]{:T(128)}, /*index=5*/bf16[64,14...) while((s32[]{:T(128)}, f32[8,4,128]{2,1,0:T(4,128)}, ...), condition=%wide.region_58.59_spmd.clone, body=%wide.region_8.58_spmd.clone.sunk | while | flops 54501536 | bytes 91818272 | solution.py:124
  301.9 25.1 %constant_dynamic-slice_fusion.50 = (bf16[64,8,4,128]{3,0,2,1:T(8,128)(2,1)}, bf16[64,8,4,128]{3,0,2,1:T(8,128)(2,1)S(1)}, bf16[64,8,4,128]{3,0,2,1:T(8,128)(2,1...) fusion(bf16[64,14,10,134]{3,0,2,1:T(8,128)(2,1)} %get-tuple-ele, ...), kind=kLoop, calls=%fused_computation.265.clone.1 | loop fusion | bytes 51380252 | tf_op jit(solution)/shard_map/while/body/eval_jaxpr/slice | solution.py:95
  327.0 11.4 %multiply_reduce_fusion.54 = (f32[8,4,128]{2,1,0:T(4,128)S(1)}, f32[8,4,128]{2,1,0:T(4,128)S(1)}, f32[8,4,128]{2,1,0:T(4,128)S(1)}, f32[8,4,128]{2,1,0:T(4,128)S...) fusion(f32[64,8,4,128]{3,2,1,0:T(4,128)S(1)} %get-tuple-element, ...), kind=kLoop, calls=%fused_computation.37.clone.1 | loop fusion | flops 13578240 | bytes 8077312 | tf_op jit(solution)/shard_map/while/body/eval_jaxpr/reduce_sum | solution.py:102
  338.4 12.7 %multiply_reduce_fusion.53 = (f32[8,4,128]{2,1,0:T(4,128)S(1)}, f32[8,4,128]{2,1,0:T(4,128)S(1)}, f32[8,4,128]{2,1,0:T(4,128)S(1)}, f32[8,4,128]{2,1,0:T(4,128)S...) fusion(f32[64,8,4,128]{3,2,1,0:T(4,128)S(1)} %get-tuple-element, ...), kind=kLoop, calls=%fused_computation.19.clone.1 | loop fusion | flops 18800640 | bytes 10780672 | tf_op jit(solution)/shard_map/while/body/eval_jaxpr/reduce_sum | solution.py:102
  351.2 12.1 %multiply_reduce_fusion.52 = (f32[8,4,128]{2,1,0:T(4,128)S(1)}, f32[8,4,128]{2,1,0:T(4,128)S(1)}, f32[8,4,128]{2,1,0:T(4,128)S(1)}, f32[8,4,128]{2,1,0:T(4,128)S...) fusion(f32[64,8,4,128]{3,2,1,0:T(4,128)S(1)} %get-tuple-element, ...), kind=kLoop, calls=%fused_computation.1.clone.1 | loop fusion | flops 18800640 | bytes 10780672 | tf_op jit(solution)/shard_map/while/body/eval_jaxpr/reduce_sum | solution.py:102
  363.7 2.1 multiply_add_fusion.4
  368.1 25.6 %constant_dynamic-slice_fusion.50 = (bf16[64,8,4,128]{3,0,2,1:T(8,128)(2,1)}, bf16[64,8,4,128]{3,0,2,1:T(8,128)(2,1)S(1)}, bf16[64,8,4,128]{3,0,2,1:T(8,128)(2,1...) fusion(bf16[64,14,10,134]{3,0,2,1:T(8,128)(2,1)} %get-tuple-ele, ...), kind=kLoop, calls=%fused_computation.265.clone.1 | loop fusion | bytes 51380252 | tf_op jit(solution)/shard_map/while/body/eval_jaxpr/slice | solution.py:95
  393.7 11.4 %multiply_reduce_fusion.54 = (f32[8,4,128]{2,1,0:T(4,128)S(1)}, f32[8,4,128]{2,1,0:T(4,128)S(1)}, f32[8,4,128]{2,1,0:T(4,128)S(1)}, f32[8,4,128]{2,1,0:T(4,128)S...) fusion(f32[64,8,4,128]{3,2,1,0:T(4,128)S(1)} %get-tuple-element, ...), kind=kLoop, calls=%fused_computation.37.clone.1 | loop fusion | flops 13578240 | bytes 8077312 | tf_op jit(solution)/shard_map/while/body/eval_jaxpr/reduce_sum | solution.py:102
  405.2 12.7 %multiply_reduce_fusion.53 = (f32[8,4,128]{2,1,0:T(4,128)S(1)}, f32[8,4,128]{2,1,0:T(4,128)S(1)}, f32[8,4,128]{2,1,0:T(4,128)S(1)}, f32[8,4,128]{2,1,0:T(4,128)S...) fusion(f32[64,8,4,128]{3,2,1,0:T(4,128)S(1)} %get-tuple-element, ...), kind=kLoop, calls=%fused_computation.19.clone.1 | loop fusion | flops 18800640 | bytes 10780672 | tf_op jit(solution)/shard_map/while/body/eval_jaxpr/reduce_sum | solution.py:102
  417.9 12.1 %multiply_reduce_fusion.52 = (f32[8,4,128]{2,1,0:T(4,128)S(1)}, f32[8,4,128]{2,1,0:T(4,128)S(1)}, f32[8,4,128]{2,1,0:T(4,128)S(1)}, f32[8,4,128]{2,1,0:T(4,128)S...) fusion(f32[64,8,4,128]{3,2,1,0:T(4,128)S(1)} %get-tuple-element, ...), kind=kLoop, calls=%fused_computation.1.clone.1 | loop fusion | flops 18800640 | bytes 10780672 | tf_op jit(solution)/shard_map/while/body/eval_jaxpr/reduce_sum | solution.py:102
  430.4 2.8 multiply_add_fusion.4
  435.6 25.8 %constant_dynamic-slice_fusion.50 = (bf16[64,8,4,128]{3,0,2,1:T(8,128)(2,1)}, bf16[64,8,4,128]{3,0,2,1:T(8,128)(2,1)S(1)}, bf16[64,8,4,128]{3,0,2,1:T(8,128)(2,1...) fusion(bf16[64,14,10,134]{3,0,2,1:T(8,128)(2,1)} %get-tuple-ele, ...), kind=kLoop, calls=%fused_computation.265.clone.1 | loop fusion | bytes 51380252 | tf_op jit(solution)/shard_map/while/body/eval_jaxpr/slice | solution.py:95
  461.4 11.4 %multiply_reduce_fusion.54 = (f32[8,4,128]{2,1,0:T(4,128)S(1)}, f32[8,4,128]{2,1,0:T(4,128)S(1)}, f32[8,4,128]{2,1,0:T(4,128)S(1)}, f32[8,4,128]{2,1,0:T(4,128)S...) fusion(f32[64,8,4,128]{3,2,1,0:T(4,128)S(1)} %get-tuple-element, ...), kind=kLoop, calls=%fused_computation.37.clone.1 | loop fusion | flops 13578240 | bytes 8077312 | tf_op jit(solution)/shard_map/while/body/eval_jaxpr/reduce_sum | solution.py:102
  472.8 12.7 %multiply_reduce_fusion.53 = (f32[8,4,128]{2,1,0:T(4,128)S(1)}, f32[8,4,128]{2,1,0:T(4,128)S(1)}, f32[8,4,128]{2,1,0:T(4,128)S(1)}, f32[8,4,128]{2,1,0:T(4,128)S...) fusion(f32[64,8,4,128]{3,2,1,0:T(4,128)S(1)} %get-tuple-element, ...), kind=kLoop, calls=%fused_computation.19.clone.1 | loop fusion | flops 18800640 | bytes 10780672 | tf_op jit(solution)/shard_map/while/body/eval_jaxpr/reduce_sum | solution.py:102
  485.6 12.1 %multiply_reduce_fusion.52 = (f32[8,4,128]{2,1,0:T(4,128)S(1)}, f32[8,4,128]{2,1,0:T(4,128)S(1)}, f32[8,4,128]{2,1,0:T(4,128)S(1)}, f32[8,4,128]{2,1,0:T(4,128)S...) fusion(f32[64,8,4,128]{3,2,1,0:T(4,128)S(1)} %get-tuple-element, ...), kind=kLoop, calls=%fused_computation.1.clone.1 | loop fusion | flops 18800640 | bytes 10780672 | tf_op jit(solution)/shard_map/while/body/eval_jaxpr/reduce_sum | solution.py:102
  498.0 2.8 multiply_add_fusion.4
  503.2 24.4 %constant_dynamic-slice_fusion.50 = (bf16[64,8,4,128]{3,0,2,1:T(8,128)(2,1)}, bf16[64,8,4,128]{3,0,2,1:T(8,128)(2,1)S(1)}, bf16[64,8,4,128]{3,0,2,1:T(8,128)(2,1...) fusion(bf16[64,14,10,134]{3,0,2,1:T(8,128)(2,1)} %get-tuple-ele, ...), kind=kLoop, calls=%fused_computation.265.clone.1 | loop fusion | bytes 51380252 | tf_op jit(solution)/shard_map/while/body/eval_jaxpr/slice | solution.py:95
  527.7 11.4 %multiply_reduce_fusion.54 = (f32[8,4,128]{2,1,0:T(4,128)S(1)}, f32[8,4,128]{2,1,0:T(4,128)S(1)}, f32[8,4,128]{2,1,0:T(4,128)S(1)}, f32[8,4,128]{2,1,0:T(4,128)S...) fusion(f32[64,8,4,128]{3,2,1,0:T(4,128)S(1)} %get-tuple-element, ...), kind=kLoop, calls=%fused_computation.37.clone.1 | loop fusion | flops 13578240 | bytes 8077312 | tf_op jit(solution)/shard_map/while/body/eval_jaxpr/reduce_sum | solution.py:102
  539.1 12.7 %multiply_reduce_fusion.53 = (f32[8,4,128]{2,1,0:T(4,128)S(1)}, f32[8,4,128]{2,1,0:T(4,128)S(1)}, f32[8,4,128]{2,1,0:T(4,128)S(1)}, f32[8,4,128]{2,1,0:T(4,128)S...) fusion(f32[64,8,4,128]{3,2,1,0:T(4,128)S(1)} %get-tuple-element, ...), kind=kLoop, calls=%fused_computation.19.clone.1 | loop fusion | flops 18800640 | bytes 10780672 | tf_op jit(solution)/shard_map/while/body/eval_jaxpr/reduce_sum | solution.py:102
  551.9 12.1 %multiply_reduce_fusion.52 = (f32[8,4,128]{2,1,0:T(4,128)S(1)}, f32[8,4,128]{2,1,0:T(4,128)S(1)}, f32[8,4,128]{2,1,0:T(4,128)S(1)}, f32[8,4,128]{2,1,0:T(4,128)S...) fusion(f32[64,8,4,128]{3,2,1,0:T(4,128)S(1)} %get-tuple-element, ...), kind=kLoop, calls=%fused_computation.1.clone.1 | loop fusion | flops 18800640 | bytes 10780672 | tf_op jit(solution)/shard_map/while/body/eval_jaxpr/reduce_sum | solution.py:102
  564.3 2.8 multiply_add_fusion.4
  569.5 24.3 %constant_dynamic-slice_fusion.50 = (bf16[64,8,4,128]{3,0,2,1:T(8,128)(2,1)}, bf16[64,8,4,128]{3,0,2,1:T(8,128)(2,1)S(1)}, bf16[64,8,4,128]{3,0,2,1:T(8,128)(2,1...) fusion(bf16[64,14,10,134]{3,0,2,1:T(8,128)(2,1)} %get-tuple-ele, ...), kind=kLoop, calls=%fused_computation.265.clone.1 | loop fusion | bytes 51380252 | tf_op jit(solution)/shard_map/while/body/eval_jaxpr/slice | solution.py:95
  593.8 11.4 %multiply_reduce_fusion.54 = (f32[8,4,128]{2,1,0:T(4,128)S(1)}, f32[8,4,128]{2,1,0:T(4,128)S(1)}, f32[8,4,128]{2,1,0:T(4,128)S(1)}, f32[8,4,128]{2,1,0:T(4,128)S...) fusion(f32[64,8,4,128]{3,2,1,0:T(4,128)S(1)} %get-tuple-element, ...), kind=kLoop, calls=%fused_computation.37.clone.1 | loop fusion | flops 13578240 | bytes 8077312 | tf_op jit(solution)/shard_map/while/body/eval_jaxpr/reduce_sum | solution.py:102
  605.2 12.7 %multiply_reduce_fusion.53 = (f32[8,4,128]{2,1,0:T(4,128)S(1)}, f32[8,4,128]{2,1,0:T(4,128)S(1)}, f32[8,4,128]{2,1,0:T(4,128)S(1)}, f32[8,4,128]{2,1,0:T(4,128)S...) fusion(f32[64,8,4,128]{3,2,1,0:T(4,128)S(1)} %get-tuple-element, ...), kind=kLoop, calls=%fused_computation.19.clone.1 | loop fusion | flops 18800640 | bytes 10780672 | tf_op jit(solution)/shard_map/while/body/eval_jaxpr/reduce_sum | solution.py:102
  618.0 12.1 %multiply_reduce_fusion.52 = (f32[8,4,128]{2,1,0:T(4,128)S(1)}, f32[8,4,128]{2,1,0:T(4,128)S(1)}, f32[8,4,128]{2,1,0:T(4,128)S(1)}, f32[8,4,128]{2,1,0:T(4,128)S...) fusion(f32[64,8,4,128]{3,2,1,0:T(4,128)S(1)} %get-tuple-element, ...), kind=kLoop, calls=%fused_computation.1.clone.1 | loop fusion | flops 18800640 | bytes 10780672 | tf_op jit(solution)/shard_map/while/body/eval_jaxpr/reduce_sum | solution.py:102
  630.5 2.8 multiply_add_fusion.4
  635.7 24.2 %constant_dynamic-slice_fusion.50 = (bf16[64,8,4,128]{3,0,2,1:T(8,128)(2,1)}, bf16[64,8,4,128]{3,0,2,1:T(8,128)(2,1)S(1)}, bf16[64,8,4,128]{3,0,2,1:T(8,128)(2,1...) fusion(bf16[64,14,10,134]{3,0,2,1:T(8,128)(2,1)} %get-tuple-ele, ...), kind=kLoop, calls=%fused_computation.265.clone.1 | loop fusion | bytes 51380252 | tf_op jit(solution)/shard_map/while/body/eval_jaxpr/slice | solution.py:95
  659.9 11.4 %multiply_reduce_fusion.54 = (f32[8,4,128]{2,1,0:T(4,128)S(1)}, f32[8,4,128]{2,1,0:T(4,128)S(1)}, f32[8,4,128]{2,1,0:T(4,128)S(1)}, f32[8,4,128]{2,1,0:T(4,128)S...) fusion(f32[64,8,4,128]{3,2,1,0:T(4,128)S(1)} %get-tuple-element, ...), kind=kLoop, calls=%fused_computation.37.clone.1 | loop fusion | flops 13578240 | bytes 8077312 | tf_op jit(solution)/shard_map/while/body/eval_jaxpr/reduce_sum | solution.py:102
  671.4 12.7 %multiply_reduce_fusion.53 = (f32[8,4,128]{2,1,0:T(4,128)S(1)}, f32[8,4,128]{2,1,0:T(4,128)S(1)}, f32[8,4,128]{2,1,0:T(4,128)S(1)}, f32[8,4,128]{2,1,0:T(4,128)S...) fusion(f32[64,8,4,128]{3,2,1,0:T(4,128)S(1)} %get-tuple-element, ...), kind=kLoop, calls=%fused_computation.19.clone.1 | loop fusion | flops 18800640 | bytes 10780672 | tf_op jit(solution)/shard_map/while/body/eval_jaxpr/reduce_sum | solution.py:102
  684.1 12.1 %multiply_reduce_fusion.52 = (f32[8,4,128]{2,1,0:T(4,128)S(1)}, f32[8,4,128]{2,1,0:T(4,128)S(1)}, f32[8,4,128]{2,1,0:T(4,128)S(1)}, f32[8,4,128]{2,1,0:T(4,128)S...) fusion(f32[64,8,4,128]{3,2,1,0:T(4,128)S(1)} %get-tuple-element, ...), kind=kLoop, calls=%fused_computation.1.clone.1 | loop fusion | flops 18800640 | bytes 10780672 | tf_op jit(solution)/shard_map/while/body/eval_jaxpr/reduce_sum | solution.py:102
  696.6 2.8 multiply_add_fusion.4
  701.8 24.2 %constant_dynamic-slice_fusion.50 = (bf16[64,8,4,128]{3,0,2,1:T(8,128)(2,1)}, bf16[64,8,4,128]{3,0,2,1:T(8,128)(2,1)S(1)}, bf16[64,8,4,128]{3,0,2,1:T(8,128)(2,1...) fusion(bf16[64,14,10,134]{3,0,2,1:T(8,128)(2,1)} %get-tuple-ele, ...), kind=kLoop, calls=%fused_computation.265.clone.1 | loop fusion | bytes 51380252 | tf_op jit(solution)/shard_map/while/body/eval_jaxpr/slice | solution.py:95
  726.0 11.4 %multiply_reduce_fusion.54 = (f32[8,4,128]{2,1,0:T(4,128)S(1)}, f32[8,4,128]{2,1,0:T(4,128)S(1)}, f32[8,4,128]{2,1,0:T(4,128)S(1)}, f32[8,4,128]{2,1,0:T(4,128)S...) fusion(f32[64,8,4,128]{3,2,1,0:T(4,128)S(1)} %get-tuple-element, ...), kind=kLoop, calls=%fused_computation.37.clone.1 | loop fusion | flops 13578240 | bytes 8077312 | tf_op jit(solution)/shard_map/while/body/eval_jaxpr/reduce_sum | solution.py:102
  737.4 12.7 %multiply_reduce_fusion.53 = (f32[8,4,128]{2,1,0:T(4,128)S(1)}, f32[8,4,128]{2,1,0:T(4,128)S(1)}, f32[8,4,128]{2,1,0:T(4,128)S(1)}, f32[8,4,128]{2,1,0:T(4,128)S...) fusion(f32[64,8,4,128]{3,2,1,0:T(4,128)S(1)} %get-tuple-element, ...), kind=kLoop, calls=%fused_computation.19.clone.1 | loop fusion | flops 18800640 | bytes 10780672 | tf_op jit(solution)/shard_map/while/body/eval_jaxpr/reduce_sum | solution.py:102
  750.2 12.1 %multiply_reduce_fusion.52 = (f32[8,4,128]{2,1,0:T(4,128)S(1)}, f32[8,4,128]{2,1,0:T(4,128)S(1)}, f32[8,4,128]{2,1,0:T(4,128)S(1)}, f32[8,4,128]{2,1,0:T(4,128)S...) fusion(f32[64,8,4,128]{3,2,1,0:T(4,128)S(1)} %get-tuple-element, ...), kind=kLoop, calls=%fused_computation.1.clone.1 | loop fusion | flops 18800640 | bytes 10780672 | tf_op jit(solution)/shard_map/while/body/eval_jaxpr/reduce_sum | solution.py:102
  762.6 2.8 multiply_add_fusion.4
  (382 shorter events, 60.7 us)
Async XLA Ops:
  0.0 20.8 %copy-start = (f32[64,1,3,3,3]{0,1,4,3,2:T(1,128)S(1)}, f32[64,1,3,3,3]{0,1,4,3,2:T(1,128)}, u32[]{:S(2)}) copy-start(f32[64,1,3,3,3]{0,1,4,3,2:T(1,128)} %param.13) | copy-start | bytes 20740
  0.0 20.9 %copy-start.21 = (pred[16,17]{0,1:T(8,128)(4,1)S(1)}, pred[16,17]{0,1:T(8,128)(4,1)}, u32[]{:S(2)}) copy-start(pred[16,17]{0,1:T(8,128)(4,1)} %constant.226) | copy-start | bytes 820
  0.8 6.4 collective-permute-start
  5.3 4.9 collective-permute-start.1
  11.0 4.5 collective-permute-start.2
  14.2 4.4 collective-permute-start.3
  44.5 71.7 %copy-start.17 = (f32[64]{0:T(128)S(1)}, f32[64]{0:T(128)}, u32[]{:S(2)}) copy-start(f32[64]{0:T(128)} %param.14) | copy-start | bytes 772
  44.5 71.7 %copy-start.18 = (f32[64]{0:T(128)S(1)}, f32[64]{0:T(128)}, u32[]{:S(2)}) copy-start(f32[64]{0:T(128)} %param.15) | copy-start | bytes 772
  122.7 8.5 %collective-permute-start.4 = (bf16[2,64,1,4,128]{1,3,4,0,2:T(4,128)(2,1)}, bf16[2,64,1,4,128]{1,3,4,0,2:T(4,128)(2,1)S(1)}, u32[]{:S(2)}, u32[]{:S(2)}) collective-permute-start(bf16[2,64,1,4,128]{1,3,4,0,2:T(4,128)(2,1)} %slice_bitcast_fusion.5), channel_id=1, source_target_pairs={{0,32},{32,64},{64,96},{1,33},{33,65},{65,97},{2,34},{34,66},{66,9... | collective-permute-start | bytes 393224 | tf_op jit(solution)/shard_map/ppermute | solution.py:16
  127.1 8.0 %collective-permute-start.5 = (bf16[2,64,1,4,128]{1,3,4,0,2:T(4,128)(2,1)}, bf16[2,64,1,4,128]{1,3,4,0,2:T(4,128)(2,1)}, u32[]{:S(2)}, u32[]{:S(2)}) collective-permute-start(bf16[2,64,1,4,128]{1,3,4,0,2:T(4,128)(2,1)} %slice_bitcast_fusion.4), channel_id=1, source_target_pairs={{32,0},{64,32},{96,64},{33,1},{65,33},{97,65},{34,2},{66,34},{98,6... | collective-permute-start | bytes 393224 | tf_op jit(solution)/shard_map/ppermute | solution.py:17
  136.2 5.4 collective-permute-start.6
  137.6 8.3 %collective-permute-start.7 = (bf16[2,64,10,1,128]{4,1,3,2,0:T(8,128)(2,1)S(1)}, bf16[2,64,10,1,128]{4,1,3,2,0:T(8,128)(2,1)}, u32[]{:S(2)}, u32[]{:S(2)}) collective-permute-start(bf16[2,64,10,1,128]{4,1,3,2,0:T(8,128)(2,1)S(1)} %get-tuple-element.524), channel_id=1, source_target_pairs={{1,0},{2,1},{3,2},{4,3},{5,4},{6,5},{7,6},{8,7},{9,8},{10,9},{11,1... | collective-permute-start | bytes 983048 | tf_op jit(solution)/shard_map/ppermute | solution.py:17
  177.1 76.2 %copy-start.19 = (f32[64]{0:T(128)S(1)}, f32[64]{0:T(128)}, u32[]{:S(2)}) copy-start(f32[64]{0:T(128)} %param.17) | copy-start | bytes 772
  177.1 76.2 %copy-start.20 = (f32[64]{0:T(128)S(1)}, f32[64]{0:T(128)}, u32[]{:S(2)}) copy-start(f32[64]{0:T(128)} %param.18) | copy-start | bytes 772
  260.5 10.3 %collective-permute-start.8 = (bf16[64,3,4,128]{0,1,3,2:T(4,128)(2,1)}, bf16[64,3,4,128]{0,1,3,2:T(4,128)(2,1)}, u32[]{:S(2)}, u32[]{:S(2)}) collective-permute-start(bf16[64,3,4,128]{0,1,3,2:T(4,128)(2,1)} %get-tuple-element.525), channel_id=1, source_target_pairs={{0,32},{32,64},{64,96},{1,33},{33,65},{65,97},{2,34},{34,66},{66,9... | collective-permute-start | bytes 589832 | tf_op jit(solution)/shard_map/ppermute | solution.py:16
  264.4 10.8 %collective-permute-start.9 = (bf16[64,3,4,128]{0,1,3,2:T(4,128)(2,1)}, bf16[64,3,4,128]{0,1,3,2:T(4,128)(2,1)}, u32[]{:S(2)}, u32[]{:S(2)}) collective-permute-start(bf16[64,3,4,128]{0,1,3,2:T(4,128)(2,1)} %get-tuple-element.526), channel_id=1, source_target_pairs={{32,0},{64,32},{96,64},{33,1},{65,33},{97,65},{34,2},{66,34},{98,6... | collective-permute-start | bytes 589832 | tf_op jit(solution)/shard_map/ppermute | solution.py:17
  279.0 11.4 %collective-permute-start.10 = (bf16[64,14,3,128]{3,0,2,1:T(8,128)(2,1)}, bf16[64,14,3,128]{3,0,2,1:T(8,128)(2,1)}, u32[]{:S(2)}, u32[]{:S(2)}) collective-permute-start(bf16[64,14,3,128]{3,0,2,1:T(8,128)(2,1)} %get-tuple-element.527), channel_id=1, source_target_pairs={{0,1},{1,2},{2,3},{3,4},{4,5},{5,6},{6,7},{7,8},{8,9},{9,10},{10,1... | collective-permute-start | bytes 2064392 | tf_op jit(solution)/shard_map/ppermute | solution.py:16
  281.2 14.2 %collective-permute-start.11 = (bf16[64,14,3,128]{3,0,2,1:T(8,128)(2,1)}, bf16[64,14,3,128]{3,0,2,1:T(8,128)(2,1)}, u32[]{:S(2)}, u32[]{:S(2)}) collective-permute-start(bf16[64,14,3,128]{3,0,2,1:T(8,128)(2,1)} %get-tuple-element.528), channel_id=1, source_target_pairs={{1,0},{2,1},{3,2},{4,3},{5,4},{6,5},{7,6},{8,7},{9,8},{10,9},{11,1... | collective-permute-start | bytes 2064392 | tf_op jit(solution)/shard_map/ppermute | solution.py:17
  351.2 12.2 %copy-start.6 = (f32[8,4,128]{2,1,0:T(4,128)S(1)}, f32[8,4,128]{2,1,0:T(4,128)}, u32[]{:S(2)}) copy-start(f32[8,4,128]{2,1,0:T(4,128)} %get-tuple-element.921) | copy-start | bytes 49156 | tf_op jit(solution)/shard_map/while
  351.2 12.2 %copy-start.7 = (f32[8,4,128]{2,1,0:T(4,128)S(1)}, f32[8,4,128]{2,1,0:T(4,128)}, u32[]{:S(2)}) copy-start(f32[8,4,128]{2,1,0:T(4,128)} %get-tuple-element.922) | copy-start | bytes 49156 | tf_op jit(solution)/shard_map/while
  351.2 12.2 %copy-start.8 = (f32[8,4,128]{2,1,0:T(4,128)S(1)}, f32[8,4,128]{2,1,0:T(4,128)}, u32[]{:S(2)}) copy-start(f32[8,4,128]{2,1,0:T(4,128)} %get-tuple-element.923) | copy-start | bytes 49156 | tf_op jit(solution)/shard_map/while
  351.2 12.2 %copy-start.9 = (f32[8,4,128]{2,1,0:T(4,128)S(1)}, f32[8,4,128]{2,1,0:T(4,128)}, u32[]{:S(2)}) copy-start(f32[8,4,128]{2,1,0:T(4,128)} %get-tuple-element.924) | copy-start | bytes 49156 | tf_op jit(solution)/shard_map/while
  351.2 12.2 %copy-start.10 = (f32[8,4,128]{2,1,0:T(4,128)S(1)}, f32[8,4,128]{2,1,0:T(4,128)}, u32[]{:S(2)}) copy-start(f32[8,4,128]{2,1,0:T(4,128)} %get-tuple-element.925) | copy-start | bytes 49156 | tf_op jit(solution)/shard_map/while
  351.2 12.2 %copy-start.11 = (f32[8,4,128]{2,1,0:T(4,128)S(1)}, f32[8,4,128]{2,1,0:T(4,128)}, u32[]{:S(2)}) copy-start(f32[8,4,128]{2,1,0:T(4,128)} %get-tuple-element.926) | copy-start | bytes 49156 | tf_op jit(solution)/shard_map/while
  351.2 12.2 %copy-start.14 = (f32[8,4,128]{2,1,0:T(4,128)S(1)}, f32[8,4,128]{2,1,0:T(4,128)}, u32[]{:S(2)}) copy-start(f32[8,4,128]{2,1,0:T(4,128)} %get-tuple-element.1159) | copy-start | bytes 49156 | tf_op jit(solution)/shard_map/while
  417.9 12.2 %copy-start.6 = (f32[8,4,128]{2,1,0:T(4,128)S(1)}, f32[8,4,128]{2,1,0:T(4,128)}, u32[]{:S(2)}) copy-start(f32[8,4,128]{2,1,0:T(4,128)} %get-tuple-element.921) | copy-start | bytes 49156 | tf_op jit(solution)/shard_map/while
  417.9 12.2 %copy-start.7 = (f32[8,4,128]{2,1,0:T(4,128)S(1)}, f32[8,4,128]{2,1,0:T(4,128)}, u32[]{:S(2)}) copy-start(f32[8,4,128]{2,1,0:T(4,128)} %get-tuple-element.922) | copy-start | bytes 49156 | tf_op jit(solution)/shard_map/while
  417.9 12.2 %copy-start.8 = (f32[8,4,128]{2,1,0:T(4,128)S(1)}, f32[8,4,128]{2,1,0:T(4,128)}, u32[]{:S(2)}) copy-start(f32[8,4,128]{2,1,0:T(4,128)} %get-tuple-element.923) | copy-start | bytes 49156 | tf_op jit(solution)/shard_map/while
  417.9 12.2 %copy-start.9 = (f32[8,4,128]{2,1,0:T(4,128)S(1)}, f32[8,4,128]{2,1,0:T(4,128)}, u32[]{:S(2)}) copy-start(f32[8,4,128]{2,1,0:T(4,128)} %get-tuple-element.924) | copy-start | bytes 49156 | tf_op jit(solution)/shard_map/while
  417.9 12.2 %copy-start.10 = (f32[8,4,128]{2,1,0:T(4,128)S(1)}, f32[8,4,128]{2,1,0:T(4,128)}, u32[]{:S(2)}) copy-start(f32[8,4,128]{2,1,0:T(4,128)} %get-tuple-element.925) | copy-start | bytes 49156 | tf_op jit(solution)/shard_map/while
  417.9 12.2 %copy-start.11 = (f32[8,4,128]{2,1,0:T(4,128)S(1)}, f32[8,4,128]{2,1,0:T(4,128)}, u32[]{:S(2)}) copy-start(f32[8,4,128]{2,1,0:T(4,128)} %get-tuple-element.926) | copy-start | bytes 49156 | tf_op jit(solution)/shard_map/while
  417.9 12.2 %copy-start.14 = (f32[8,4,128]{2,1,0:T(4,128)S(1)}, f32[8,4,128]{2,1,0:T(4,128)}, u32[]{:S(2)}) copy-start(f32[8,4,128]{2,1,0:T(4,128)} %get-tuple-element.1159) | copy-start | bytes 49156 | tf_op jit(solution)/shard_map/while
  485.5 12.2 %copy-start.6 = (f32[8,4,128]{2,1,0:T(4,128)S(1)}, f32[8,4,128]{2,1,0:T(4,128)}, u32[]{:S(2)}) copy-start(f32[8,4,128]{2,1,0:T(4,128)} %get-tuple-element.921) | copy-start | bytes 49156 | tf_op jit(solution)/shard_map/while
  485.5 12.2 %copy-start.7 = (f32[8,4,128]{2,1,0:T(4,128)S(1)}, f32[8,4,128]{2,1,0:T(4,128)}, u32[]{:S(2)}) copy-start(f32[8,4,128]{2,1,0:T(4,128)} %get-tuple-element.922) | copy-start | bytes 49156 | tf_op jit(solution)/shard_map/while
  485.5 12.2 %copy-start.8 = (f32[8,4,128]{2,1,0:T(4,128)S(1)}, f32[8,4,128]{2,1,0:T(4,128)}, u32[]{:S(2)}) copy-start(f32[8,4,128]{2,1,0:T(4,128)} %get-tuple-element.923) | copy-start | bytes 49156 | tf_op jit(solution)/shard_map/while
  485.5 12.2 %copy-start.9 = (f32[8,4,128]{2,1,0:T(4,128)S(1)}, f32[8,4,128]{2,1,0:T(4,128)}, u32[]{:S(2)}) copy-start(f32[8,4,128]{2,1,0:T(4,128)} %get-tuple-element.924) | copy-start | bytes 49156 | tf_op jit(solution)/shard_map/while
  485.6 12.2 %copy-start.10 = (f32[8,4,128]{2,1,0:T(4,128)S(1)}, f32[8,4,128]{2,1,0:T(4,128)}, u32[]{:S(2)}) copy-start(f32[8,4,128]{2,1,0:T(4,128)} %get-tuple-element.925) | copy-start | bytes 49156 | tf_op jit(solution)/shard_map/while
  485.6 12.2 %copy-start.11 = (f32[8,4,128]{2,1,0:T(4,128)S(1)}, f32[8,4,128]{2,1,0:T(4,128)}, u32[]{:S(2)}) copy-start(f32[8,4,128]{2,1,0:T(4,128)} %get-tuple-element.926) | copy-start | bytes 49156 | tf_op jit(solution)/shard_map/while
  485.6 12.2 %copy-start.14 = (f32[8,4,128]{2,1,0:T(4,128)S(1)}, f32[8,4,128]{2,1,0:T(4,128)}, u32[]{:S(2)}) copy-start(f32[8,4,128]{2,1,0:T(4,128)} %get-tuple-element.1159) | copy-start | bytes 49156 | tf_op jit(solution)/shard_map/while
  551.8 12.2 %copy-start.6 = (f32[8,4,128]{2,1,0:T(4,128)S(1)}, f32[8,4,128]{2,1,0:T(4,128)}, u32[]{:S(2)}) copy-start(f32[8,4,128]{2,1,0:T(4,128)} %get-tuple-element.921) | copy-start | bytes 49156 | tf_op jit(solution)/shard_map/while
  551.8 12.2 %copy-start.7 = (f32[8,4,128]{2,1,0:T(4,128)S(1)}, f32[8,4,128]{2,1,0:T(4,128)}, u32[]{:S(2)}) copy-start(f32[8,4,128]{2,1,0:T(4,128)} %get-tuple-element.922) | copy-start | bytes 49156 | tf_op jit(solution)/shard_map/while
  551.8 12.2 %copy-start.8 = (f32[8,4,128]{2,1,0:T(4,128)S(1)}, f32[8,4,128]{2,1,0:T(4,128)}, u32[]{:S(2)}) copy-start(f32[8,4,128]{2,1,0:T(4,128)} %get-tuple-element.923) | copy-start | bytes 49156 | tf_op jit(solution)/shard_map/while
  551.8 12.2 %copy-start.9 = (f32[8,4,128]{2,1,0:T(4,128)S(1)}, f32[8,4,128]{2,1,0:T(4,128)}, u32[]{:S(2)}) copy-start(f32[8,4,128]{2,1,0:T(4,128)} %get-tuple-element.924) | copy-start | bytes 49156 | tf_op jit(solution)/shard_map/while
  551.8 12.2 %copy-start.10 = (f32[8,4,128]{2,1,0:T(4,128)S(1)}, f32[8,4,128]{2,1,0:T(4,128)}, u32[]{:S(2)}) copy-start(f32[8,4,128]{2,1,0:T(4,128)} %get-tuple-element.925) | copy-start | bytes 49156 | tf_op jit(solution)/shard_map/while
  551.8 12.2 %copy-start.11 = (f32[8,4,128]{2,1,0:T(4,128)S(1)}, f32[8,4,128]{2,1,0:T(4,128)}, u32[]{:S(2)}) copy-start(f32[8,4,128]{2,1,0:T(4,128)} %get-tuple-element.926) | copy-start | bytes 49156 | tf_op jit(solution)/shard_map/while
  551.9 12.2 %copy-start.14 = (f32[8,4,128]{2,1,0:T(4,128)S(1)}, f32[8,4,128]{2,1,0:T(4,128)}, u32[]{:S(2)}) copy-start(f32[8,4,128]{2,1,0:T(4,128)} %get-tuple-element.1159) | copy-start | bytes 49156 | tf_op jit(solution)/shard_map/while
  618.0 12.2 %copy-start.7 = (f32[8,4,128]{2,1,0:T(4,128)S(1)}, f32[8,4,128]{2,1,0:T(4,128)}, u32[]{:S(2)}) copy-start(f32[8,4,128]{2,1,0:T(4,128)} %get-tuple-element.922) | copy-start | bytes 49156 | tf_op jit(solution)/shard_map/while
  618.0 12.2 %copy-start.8 = (f32[8,4,128]{2,1,0:T(4,128)S(1)}, f32[8,4,128]{2,1,0:T(4,128)}, u32[]{:S(2)}) copy-start(f32[8,4,128]{2,1,0:T(4,128)} %get-tuple-element.923) | copy-start | bytes 49156 | tf_op jit(solution)/shard_map/while
  618.0 12.2 %copy-start.9 = (f32[8,4,128]{2,1,0:T(4,128)S(1)}, f32[8,4,128]{2,1,0:T(4,128)}, u32[]{:S(2)}) copy-start(f32[8,4,128]{2,1,0:T(4,128)} %get-tuple-element.924) | copy-start | bytes 49156 | tf_op jit(solution)/shard_map/while
  618.0 12.2 %copy-start.10 = (f32[8,4,128]{2,1,0:T(4,128)S(1)}, f32[8,4,128]{2,1,0:T(4,128)}, u32[]{:S(2)}) copy-start(f32[8,4,128]{2,1,0:T(4,128)} %get-tuple-element.925) | copy-start | bytes 49156 | tf_op jit(solution)/shard_map/while
  618.0 12.2 %copy-start.11 = (f32[8,4,128]{2,1,0:T(4,128)S(1)}, f32[8,4,128]{2,1,0:T(4,128)}, u32[]{:S(2)}) copy-start(f32[8,4,128]{2,1,0:T(4,128)} %get-tuple-element.926) | copy-start | bytes 49156 | tf_op jit(solution)/shard_map/while
  618.0 12.2 %copy-start.14 = (f32[8,4,128]{2,1,0:T(4,128)S(1)}, f32[8,4,128]{2,1,0:T(4,128)}, u32[]{:S(2)}) copy-start(f32[8,4,128]{2,1,0:T(4,128)} %get-tuple-element.1159) | copy-start | bytes 49156 | tf_op jit(solution)/shard_map/while
  684.1 12.2 %copy-start.7 = (f32[8,4,128]{2,1,0:T(4,128)S(1)}, f32[8,4,128]{2,1,0:T(4,128)}, u32[]{:S(2)}) copy-start(f32[8,4,128]{2,1,0:T(4,128)} %get-tuple-element.922) | copy-start | bytes 49156 | tf_op jit(solution)/shard_map/while
  684.1 12.2 %copy-start.8 = (f32[8,4,128]{2,1,0:T(4,128)S(1)}, f32[8,4,128]{2,1,0:T(4,128)}, u32[]{:S(2)}) copy-start(f32[8,4,128]{2,1,0:T(4,128)} %get-tuple-element.923) | copy-start | bytes 49156 | tf_op jit(solution)/shard_map/while
  684.1 12.2 %copy-start.9 = (f32[8,4,128]{2,1,0:T(4,128)S(1)}, f32[8,4,128]{2,1,0:T(4,128)}, u32[]{:S(2)}) copy-start(f32[8,4,128]{2,1,0:T(4,128)} %get-tuple-element.924) | copy-start | bytes 49156 | tf_op jit(solution)/shard_map/while
  684.1 12.2 %copy-start.10 = (f32[8,4,128]{2,1,0:T(4,128)S(1)}, f32[8,4,128]{2,1,0:T(4,128)}, u32[]{:S(2)}) copy-start(f32[8,4,128]{2,1,0:T(4,128)} %get-tuple-element.925) | copy-start | bytes 49156 | tf_op jit(solution)/shard_map/while
  684.1 12.2 %copy-start.11 = (f32[8,4,128]{2,1,0:T(4,128)S(1)}, f32[8,4,128]{2,1,0:T(4,128)}, u32[]{:S(2)}) copy-start(f32[8,4,128]{2,1,0:T(4,128)} %get-tuple-element.926) | copy-start | bytes 49156 | tf_op jit(solution)/shard_map/while
  684.1 12.2 %copy-start.14 = (f32[8,4,128]{2,1,0:T(4,128)S(1)}, f32[8,4,128]{2,1,0:T(4,128)}, u32[]{:S(2)}) copy-start(f32[8,4,128]{2,1,0:T(4,128)} %get-tuple-element.1159) | copy-start | bytes 49156 | tf_op jit(solution)/shard_map/while
  750.1 12.2 %copy-start.7 = (f32[8,4,128]{2,1,0:T(4,128)S(1)}, f32[8,4,128]{2,1,0:T(4,128)}, u32[]{:S(2)}) copy-start(f32[8,4,128]{2,1,0:T(4,128)} %get-tuple-element.922) | copy-start | bytes 49156 | tf_op jit(solution)/shard_map/while
  750.1 12.2 %copy-start.8 = (f32[8,4,128]{2,1,0:T(4,128)S(1)}, f32[8,4,128]{2,1,0:T(4,128)}, u32[]{:S(2)}) copy-start(f32[8,4,128]{2,1,0:T(4,128)} %get-tuple-element.923) | copy-start | bytes 49156 | tf_op jit(solution)/shard_map/while
  750.1 12.2 %copy-start.9 = (f32[8,4,128]{2,1,0:T(4,128)S(1)}, f32[8,4,128]{2,1,0:T(4,128)}, u32[]{:S(2)}) copy-start(f32[8,4,128]{2,1,0:T(4,128)} %get-tuple-element.924) | copy-start | bytes 49156 | tf_op jit(solution)/shard_map/while
  750.1 12.2 %copy-start.10 = (f32[8,4,128]{2,1,0:T(4,128)S(1)}, f32[8,4,128]{2,1,0:T(4,128)}, u32[]{:S(2)}) copy-start(f32[8,4,128]{2,1,0:T(4,128)} %get-tuple-element.925) | copy-start | bytes 49156 | tf_op jit(solution)/shard_map/while
  750.2 12.2 %copy-start.11 = (f32[8,4,128]{2,1,0:T(4,128)S(1)}, f32[8,4,128]{2,1,0:T(4,128)}, u32[]{:S(2)}) copy-start(f32[8,4,128]{2,1,0:T(4,128)} %get-tuple-element.926) | copy-start | bytes 49156 | tf_op jit(solution)/shard_map/while
  750.2 12.2 %copy-start.14 = (f32[8,4,128]{2,1,0:T(4,128)S(1)}, f32[8,4,128]{2,1,0:T(4,128)}, u32[]{:S(2)}) copy-start(f32[8,4,128]{2,1,0:T(4,128)} %get-tuple-element.1159) | copy-start | bytes 49156 | tf_op jit(solution)/shard_map/while
  (40 other events, 250.2 us)
where the time goes:
time: 783 us; the launch traced here: 769 us
  other arithmetic  310 us (40%)
  local copies, waits for them, and re-layouts  226 us (29%)
  blocking collectives  144 us (18%)
  waiting for transfers between devices  30.9 us (4%)
  starting transfers between devices  28.5 us (4%)
  matrix products  27 us (3%)
    reduce_sum x21, other arithmetic, depth_step(): scores = -factor * jnp.sum(difference * difference, axis=0)  254 us
    slice x7, local copies, waits for them, and re-layouts, depth_step(): depth_plane[:, :, height_shift:height_shift + strip_cells, width_shift:wi...  174 us
    psum x1, blocking collectives, local(): lax.psum((jnp.sum(second_raw, axis=(2, 3, 4)), jnp.sum(second_raw * secon...  72.6 us
    psum x1, blocking collectives, local(): lax.psum((jnp.sum(first_raw, axis=(2, 3, 4)), jnp.sum(first_raw * first_r...  71.1 us
    conv_general_dilated x2, matrix products, convolve_valid(): lax.conv_general_dilated(field, kernel, (1, 1, 1), 'VALID', dimension_num...  27 us
    ppermute x6, waiting for transfers between devices, extended(): after = lax.ppermute(first, axis, down)  21.4 us
    add x7, other arithmetic, depth_step(): running_sum = running_sum * keep + weights  18.9 us
    ppermute x6, starting transfers between devices, extended(): before = lax.ppermute(last, axis, up)  18.5 us
  transfers between devices with their start and end apart: 12, of which 9 were waited for; matrix products, arithmetic and copies ran while one was open for 1% of the time, Pallas kernels for 0%

commit v1 on v0

v1 whole, which is shorter than its diff:
```python
import math

import jax
import jax.numpy as jnp
from jax import lax
from jax.experimental import pallas as pl
from jax.experimental.pallas import tpu as pltpu
from jax.sharding import PartitionSpec as P

MESH = pl.DeviceIdType.MESH
F32, BF16, I32 = jnp.float32, jnp.bfloat16, jnp.int32
BIG = 1e30
CELLS = 32 * 128 * 128
HALO = [(dd, hh) for hh in (-2, -1, 0, 1, 2) for dd in (-1, 0, 1) if (dd, hh) != (0, 0)]
HEIGHT_SPAN = {0: (0, 4, 5), 1: (0, 4, 1), 2: (3, 4, 0), -1: (0, 4, 9), -2: (0, 1, 13)}


def iota(shape, dim):
    return lax.broadcasted_iota(I32, shape, dim)


def dot(a, b):
    return jnp.dot(a, b, preferred_element_type=F32)


def dot_nt(a, b):
    return lax.dot_general(a, b, (((1,), (1,)), ((), ())), preferred_element_type=F32)


def rows_sum(x):
    return jnp.sum(x.reshape(x.shape[0] // 8, 8, x.shape[1]), axis=0)


def position():
    depth, height = lax.axis_index("depth"), lax.axis_index("height")
    return depth, height


def group_peers(depth, height):
    x_hi, z, y = height // 16, (height // 4) % 4, height % 4
    along_x, along_y, along_z = [], [], []
    for k in range(1, 8):
        g = (x_hi * 4 + depth + k) % 8
        along_x.append((g % 4, (g // 4) * 16 + z * 4 + y))
    for k in range(1, 4):
        along_y.append((depth, x_hi * 16 + z * 4 + (y + k) % 4))
        along_z.append((depth, x_hi * 16 + ((z + k) % 4) * 4 + y))
    return along_x, along_y, along_z


def halo_peers(depth, height):
    return [((depth + dd + 4) % 4, (height + hh + 32) % 32) for dd, hh in HALO]


def total_over_devices(value, peers, bufs, send_sems, recv_sems, works):
    count = 0
    for group, buf, work in zip(peers, bufs, works):
        buf[0] = value
        copies = []
        for k, peer in enumerate(group):
            copy = pltpu.make_async_remote_copy(
                src_ref=buf.at[0],
                dst_ref=buf.at[k + 1],
                send_sem=send_sems.at[count],
                recv_sem=recv_sems.at[count],
                device_id=peer,
                device_id_type=MESH,
            )
            copy.start()
            copies.append(copy)
            count += 1
        work()
        for copy in copies:
            copy.wait()
        value = jnp.sum(buf[...], axis=0)
    return value


def leaky(v):
    return jnp.maximum(v, 0.01 * v)


def kernel(
    fi, mi, c1, g1, s1, c2, g2, s2, sharp,
    out,
    own, ext, selm, wf, wbig, w1, v, vs, raw1f, raw1m, wmask, xf, xm,
    raw2f, raw2m, ff, kf, kb, ke, qe, sbuf, res,
    ax1, ay1, az1, ax2, ay2, az2,
    hs, hr, as1, ar1, as2, ar2,
):
    depth, height = position()
    halo = halo_peers(depth, height)
    peers = group_peers(depth, height)

    barrier = pltpu.get_barrier_semaphore()
    everyone = halo + peers[0] + peers[1] + peers[2]
    for peer in everyone:
        pl.semaphore_signal(barrier, inc=1, device_id=peer, device_id_type=MESH)
    for h in range(4):
        own[h, 0] = fi[:, h, :]
        own[h, 1] = mi[:, h, :]
    k_i, n_i = iota((512, 1024), 0), iota((512, 1024), 1)
    hit = jnp.logical_and(
        k_i // 128 == (n_i // 32) % 4, k_i % 128 == 4 * (n_i % 32) - 2 + n_i // 128
    )
    selm[...] = jnp.where(hit, 1.0, 0.0).astype(BF16)
    pl.semaphore_wait(barrier, len(everyone))

    copies = []
    for n, (dd, hh) in enumerate(HALO):
        h0, h1, land = HEIGHT_SPAN[hh]
        block = 8 - 8 * dd
        copy = pltpu.make_async_remote_copy(
            src_ref=own.at[pl.ds(h0, h1 - h0)],
            dst_ref=ext.at[pl.ds(land, h1 - h0), :, pl.ds(block, 8), :],
            send_sem=hs.at[n],
            recv_sem=hr.at[n],
            device_id=halo[n],
            device_id_type=MESH,
        )
        copy.start()
        copies.append(copy)

    ext[5:9, :, 8:16, :] = own[...]
    for pair in range(32):
        wf[pl.ds(pair, 27, stride=32), :] = c2[:, pair * 128 : (pair + 1) * 128].astype(F32)

    def build(ab, carry):
        zero = jnp.zeros((64, 64), F32)
        taps = []
        for c in range(3):
            t = wf[pl.ds(pl.multiple_of((ab * 3 + c) * 32, 32), 32), :]
            taps.append(jnp.concatenate([t[:, :64], t[:, 64:]], axis=0))
        for u in range(6):
            parts = [taps[u - wo] if 0 <= u - wo <= 2 else zero for wo in range(4)]
            row = jnp.concatenate(parts, axis=1).astype(BF16)
            wbig[pl.ds(pl.multiple_of((ab * 6 + u) * 64, 64), 64), :] = row
        return carry

    lax.fori_loop(0, 9, build, 0)

    c1p = jnp.concatenate([c1[pl.ds(0, 32, stride=2), :], c1[pl.ds(1, 32, stride=2), :]], axis=0)
    c1t = jnp.transpose(c1p)
    c1t = c1t[:32]
    zero = jnp.zeros((32, 64), F32)
    spread = jnp.concatenate(
        [jnp.concatenate([c1t if q == u else zero for q in range(6)], axis=1) for u in range(6)],
        axis=0,
    )
    spread_hi = spread.astype(BF16)
    spread_lo = (spread - spread_hi.astype(F32)).astype(BF16)
    r_i, k_i = iota((72, 192), 0), iota((72, 192), 1)
    tap = k_i % 32
    hit = jnp.logical_and(
        tap // 3 == ((r_i // 8) % 3) * 3 + r_i // 24,
        jnp.logical_and(r_i % 8 - k_i // 32 == tap % 3, tap < 27),
    )
    pick = jnp.where(hit, 1.0, 0.0).astype(BF16)
    w1_hi, w1_lo = dot(pick, spread_hi), dot(pick, spread_lo)
    w1[...] = jnp.concatenate([w1_hi, w1_hi, w1_lo], axis=0).astype(BF16)

    row, lane = iota((384, 128), 0), iota((384, 128), 1)
    gh = height * 4 - 4 + row // 32
    inside = jnp.logical_and(gh >= 0, gh < 128)
    wmask[0] = jnp.where(
        jnp.logical_and(inside, jnp.logical_or(row % 32 > 0, lane >= 64)), 1.0, 0.0
    )
    wmask[1] = jnp.where(inside, 1.0, 0.0)
    wmask[2] = jnp.where(
        jnp.logical_and(inside, jnp.logical_or(row % 32 < 31, lane < 64)), 1.0, 0.0
    )
    q_i, lane = iota((256, 128), 0), iota((256, 128), 1)
    w_q = 4 * ((q_i // 32) % 2) + q_i // 64
    for odd in range(2):
        for phase in range(4):
            w_k = 4 * ((lane - 24 - 2 * odd + 8) % 4 - 1) + phase
            far = jnp.abs(w_k - w_q) > 3
            e = jnp.where(jnp.logical_and(lane < 12, lane // 3 == phase), -1.0, 0.0)
            e = jnp.where(lane - 12 == (q_i // 4) % 8, 1.0, e)
            e = jnp.where(jnp.logical_and(lane >= 20, lane - 20 == q_i % 4), 1.0, e)
            in_quad = jnp.logical_and(lane >= 24, lane < 28)
            e = jnp.where(jnp.logical_and(in_quad, far), -BIG, e)
            qe[odd, phase] = e.astype(BF16)
    kf[...] = jnp.zeros_like(kf)

    for copy in copies:
        copy.wait()

    row = iota((48, 128), 0)
    gd = depth * 8 - 8 + row % 24
    d_in = jnp.logical_and(gd >= 0, gd < 32)
    stacks = []
    for h4 in range(4):
        parts = []
        for hh in range(4):
            hx = h4 * 4 + hh
            if hx >= 14:
                parts.append(jnp.zeros((96, 128), BF16))
                continue
            x = ext[hx].reshape(48, 128)
            gh = jnp.full((48, 128), height * 4 - 5 + hx, I32)
            ok = jnp.logical_and(d_in, jnp.logical_and(gh >= 0, gh < 128))
            x = jnp.where(ok, x, 0.0)
            hi = x.astype(BF16)
            lo = (x - hi.astype(F32)).astype(BF16)
            parts.append(jnp.concatenate([hi, lo], axis=0))
        stacks.append(jnp.concatenate(parts, axis=1))
    for h4 in range(4):
        picked = dot(stacks[h4], selm[...])
        for q in range(4):
            for j in range(8):
                v[q, h4, pl.ds(j, 24, stride=8), :] = picked[
                    q * 24 : q * 24 + 24, j * 128 : (j + 1) * 128
                ]
    for q in range(4):
        full = jnp.concatenate([v[q, h4] for h4 in range(4)], axis=1)
        for b in range(3):
            vs[b, q] = full[:, 32 * b : 32 * b + 384]

    def patches(image, dx, lane0, lanes):
        start = pl.multiple_of((dx + 3) * 8, 8)
        parts = [
            vs[b, hl * 2 + image, pl.ds(start, 24), lane0 : lane0 + lanes]
            for hl in (0, 1, 0)
            for b in range(3)
        ]
        return jnp.transpose(jnp.concatenate(parts, axis=0)).astype(BF16)

    def own_sums(dx, sums):
        result = []
        for image in range(2):
            raw = dot(patches(image, dx, 128, 128), w1[...])
            result.append(sums[2 * image] + rows_sum(raw))
            result.append(sums[2 * image + 1] + rows_sum(raw * raw))
        return tuple(result)

    start = tuple(jnp.zeros((8, 384), F32) for _ in range(4))
    sums = lax.fori_loop(4, 12, own_sums, start)

    def per_channel(s):
        s = jnp.sum(s, axis=0, keepdims=True)
        return s[:, 64:128] + s[:, 128:192] + s[:, 192:256] + s[:, 256:320]

    def stat_tile(sum_f, sq_f, sum_m, sq_m):
        return jnp.concatenate(
            [
                jnp.concatenate([sum_f, sum_m], axis=1),
                jnp.concatenate([sq_f, sq_m], axis=1),
                jnp.zeros((6, 128), F32),
            ],
            axis=0,
        )

    tile = stat_tile(*[per_channel(s) for s in sums])

    def raw_fixed():
        def step(dx, carry):
            p = patches(0, dx, 0, 384)
            raw1f[dx - 3] = dot(p[96:288], w1[...])
            return carry

        lax.fori_loop(3, 13, step, 0)

    def raw_moving(d0, d1):
        def step(dx, carry):
            raw1m[dx] = dot(patches(1, dx, 0, 384), w1[...])
            return carry

        lax.fori_loop(d0, d1, step, 0)

    tile = total_over_devices(
        tile, peers, (ax1, ay1, az1), as1, ar1,
        (raw_fixed, lambda: raw_moving(0, 8), lambda: raw_moving(8, 16)),
    )

    def scale_and_offset(tile, gain, shift):
        mean = tile[0:1] / CELLS
        mean_sq = tile[1:2] / CELLS
        inv_dev = lax.rsqrt(mean_sq - mean * mean + 1e-05)
        scale = inv_dev * gain
        offset = shift - mean * scale
        pairs = []
        for image in range(2):
            half = slice(image * 64, image * 64 + 64)
            pairs.append(
                tuple(jnp.concatenate([a[:, half], a[:, half]], axis=1) for a in (scale, offset))
            )
        return pairs

    i_i, o_i = iota((64, 128), 0), iota((64, 128), 1) % 64
    perm = jnp.where(i_i == 2 * (o_i % 32) + o_i // 32, 1.0, 0.0)
    gains = jnp.concatenate([g1[...], s1[...], jnp.zeros((6, 64), F32)], axis=0)
    gains = jnp.dot(gains, perm, preferred_element_type=F32, precision=lax.Precision.HIGHEST)
    pairs = scale_and_offset(tile, gains[0:1], gains[1:2])

    def depth_inside(d):
        g = depth * 8 + d
        return jnp.where(jnp.logical_and(g >= 0, g < 32), 1.0, 0.0)

    def feat(raw, x, image, dx, out_dx, rows):
        keep = depth_inside(dx - 4)
        scale, offset = pairs[image][0] * keep, pairs[image][1] * keep
        for s in range(3):
            y = leaky(raw[out_dx, :, s * 128 : (s + 1) * 128] * scale + offset)
            x[s, out_dx] = (y * wmask[s, rows]).astype(BF16)

    def feat_fixed(dx, carry):
        feat(raw1f, xf, 0, dx, dx - 3, slice(96, 288))
        return carry

    def feat_moving(dx, carry):
        feat(raw1m, xm, 1, dx, dx, slice(0, 384))
        return carry

    lax.fori_loop(3, 13, feat_fixed, 0)
    lax.fori_loop(0, 16, feat_moving, 0)

    def second(x, od, spans):
        parts = []
        for a in range(3):
            for b in range(3):
                for s in range(3):
                    got = [x[s, od + a, (h + b) * 32 : (h + b + n) * 32, :] for h, n in spans]
                    parts.append(got[0] if len(got) == 1 else jnp.concatenate(got, axis=0))
        return dot(jnp.concatenate(parts, axis=1), wbig[...])

    def own_second(d, sums):
        raw_f = second(xf, d, ((0, 4),))
        raw2f[d] = raw_f
        raw_m = second(xm, d + 3, ((3, 4),))
        raw2m[d + 3, 96:224, :] = raw_m
        return (
            sums[0] + rows_sum(raw_f),
            sums[1] + rows_sum(raw_f * raw_f),
            sums[2] + rows_sum(raw_m),
            sums[3] + rows_sum(raw_m * raw_m),
        )

    start = tuple(jnp.zeros((8, 256), F32) for _ in range(4))
    sums = lax.fori_loop(0, 8, own_second, start)

    def per_channel_two(s):
        s = jnp.sum(s, axis=0, keepdims=True)
        return s[:, :64] + s[:, 64:128] + s[:, 128:192] + s[:, 192:]

    tile = stat_tile(*[per_channel_two(s) for s in sums])

    def planes(d0, d1):
        def step(od, carry):
            raw2m[od] = second(xm, od, ((0, 10),))
            return carry

        lax.fori_loop(d0, d1, step, 0)

    def sides():
        def step(od, carry):
            raw = second(xm, od, ((0, 3), (7, 3)))
            raw2m[od, 0:96, :] = raw[:96]
            raw2m[od, 224:320, :] = raw[96:]
            return carry

        lax.fori_loop(3, 11, step, 0)

    tile = total_over_devices(
        tile, peers, (ax2, ay2, az2), as2, ar2,
        (lambda: planes(0, 3), lambda: planes(11, 14), sides),
    )
    gain2 = jnp.concatenate([g2[...], g2[...]], axis=1)
    shift2 = jnp.concatenate([s2[...], s2[...]], axis=1)
    pairs2 = scale_and_offset(tile, gain2, shift2)

    def rounded(y):
        return leaky(y).astype(BF16).astype(F32)

    def spread_fixed(d, carry):
        scale, offset = pairs2[0]
        for h in range(4):
            for c in range(2):
                y = raw2f[d, h * 32 : (h + 1) * 32, c * 128 : (c + 1) * 128] * scale + offset
                ff[c, pl.ds(d * 4 + h, 32, stride=32), :] = rounded(y)
        return carry

    lax.fori_loop(0, 8, spread_fixed, 0)

    def spread_moving(od, carry):
        keep_d = depth_inside(od - 3)
        for oh in range(10):
            gh = height * 4 - 3 + oh
            keep = jnp.where(jnp.logical_and(gh >= 0, gh < 128), keep_d, 0.0)
            scale, offset = pairs2[1][0] * keep, pairs2[1][1] * keep
            for c in range(2):
                y = raw2m[od, oh * 32 : (oh + 1) * 32, c * 128 : (c + 1) * 128] * scale + offset
                kf[c, pl.ds(160 + oh * 16 + od, 32, stride=160), :] = rounded(y)
        return carry

    lax.fori_loop(0, 14, spread_moving, 0)

    k_i, n_i = iota((512, 128), 0), iota((512, 128), 1)
    hit = jnp.logical_and(
        n_i < 12, (k_i // 256) * 2 + (k_i % 128) // 64 == n_i // 3
    )
    ones = jnp.where(hit, 1.0, 0.0).astype(BF16)
    row, lane = iota((160, 128), 0), iota((160, 128), 1)
    dd, hh = row % 16 - (lane - 12), row // 16 - (lane - 20)
    bad_d = jnp.logical_and(
        jnp.logical_and(lane >= 12, lane < 20), jnp.logical_or(dd < 0, dd > 6)
    )
    bad_h = jnp.logical_and(
        jnp.logical_and(lane >= 20, lane < 24), jnp.logical_or(hh < 0, hh > 6)
    )
    base = jnp.where(jnp.logical_or(bad_d, bad_h), -BIG, 0.0)
    third = lane % 3

    def keys(q, carry):
        at = pl.ds(pl.multiple_of(q * 160, 160), 160)
        squares = []
        for c in range(2):
            m = kf[c, at, :]
            kb[c, at, :] = m.astype(BF16)
            sq = m * m
            hi = sq.astype(BF16)
            squares += [hi, (sq - hi.astype(F32)).astype(BF16)]
        norm = dot(jnp.concatenate(squares, axis=1), ones)
        hi = norm.astype(BF16).astype(F32)
        rest = norm - hi
        mid = rest.astype(BF16).astype(F32)
        term = jnp.where(third == 0, hi, jnp.where(third == 1, mid, rest - mid))
        e = jnp.where(lane == 24 + q % 4, 1.0, base)
        ke[at, :] = jnp.where(lane < 12, term, e).astype(BF16)
        return carry

    lax.fori_loop(0, 34, keys, 0)

    rate = sharp[0] * (math.log2(math.e) / 64.0)
    low = iota((64, 128), 1) < 64
    sub = iota((8, 256), 0).astype(F32)
    n_i = iota((1, 256), 1)
    q_w = (4 * ((n_i // 32) % 2) + n_i // 64).astype(F32)
    q_d = ((n_i // 4) % 8).astype(F32)
    q_h = (n_i % 4).astype(F32)
    tiles = [(phase, rel) for phase in range(4) for rel in range(4)
             if (phase, rel) not in ((0, 0), (3, 3))]

    def block(R, carry):
        at = pl.ds(pl.multiple_of(R * 64, 64), 64)
        a, b = 2.0 * ff[0, at, :], 2.0 * ff[1, at, :]
        ra, rb = pltpu.roll(a, 64, 1), pltpu.roll(b, 64, 1)
        first = jnp.concatenate([jnp.where(low, t, 0.0) for t in (a, ra, b, rb)], axis=0)
        second_ = jnp.concatenate([jnp.where(low, 0.0, t) for t in (ra, a, rb, b)], axis=0)
        query = (first.astype(BF16), second_.astype(BF16))
        odd = R % 2
        best = jnp.full((8, 256), -jnp.inf, F32)
        for phase in range(4):
            rels = [rel for p, rel in tiles if p == phase]
            count = len(rels) * 160
            rows = pl.ds(pl.multiple_of((2 * R + rels[0]) * 160, 160), count)
            lhs = jnp.concatenate([kb[phase // 2, rows, :], ke[rows, :]], axis=1)
            rhs = jnp.concatenate([query[phase % 2], qe[odd, phase]], axis=1)
            score = dot_nt(lhs, rhs)
            place = tiles.index((phase, rels[0])) * 160
            sbuf[place : place + count, :] = score
            best = jnp.maximum(best, jnp.max(score.reshape(count // 8, 8, 256), axis=0))
        top = jnp.broadcast_to(jnp.max(best, axis=0, keepdims=True), (8, 256))
        zero = jnp.zeros((8, 256), F32)
        by_h = [zero] * 10
        upper, total, w_sum = zero, zero, zero
        for n, (phase, rel) in enumerate(tiles):
            tile_sum = zero
            for oh in range(10):
                at_row = n * 160 + oh * 16
                p0 = jnp.exp2((sbuf[at_row : at_row + 8, :] - top) * rate)
                p1 = jnp.exp2((sbuf[at_row + 8 : at_row + 16, :] - top) * rate)
                both = p0 + p1
                upper = upper + p1
                by_h[oh] = by_h[oh] + both
                tile_sum = tile_sum + both
            total = total + tile_sum
            w_sum = w_sum + tile_sum * float(4 * (rel - 1) + phase)
        h_sum = zero
        for oh in range(1, 10):
            h_sum = h_sum + by_h[oh] * float(oh)
        d_sum = total * sub + 8.0 * upper
        weight = jnp.sum(total, axis=0, keepdims=True)

        def mean(s):
            return jnp.sum(s, axis=0, keepdims=True) / weight

        res[0, pl.ds(R, 1), :] = mean(d_sum) - (q_d + 3.0)
        res[1, pl.ds(R, 1), :] = mean(h_sum) - (q_h + 3.0)
        res[2, pl.ds(R, 1), :] = mean(w_sum) - q_w
        return carry

    lax.fori_loop(0, 16, block, 0)

    k_i, w_i = iota((128, 128), 0), iota((128, 128), 1)
    g, blk = k_i // 16, k_i % 16
    order = jnp.where(w_i == blk * 8 + (g % 2) * 4 + g // 2, 1.0, 0.0)
    for component in range(3):
        t = jnp.transpose(res[component])
        t = jnp.concatenate([t[n * 32 : (n + 1) * 32] for n in range(8)], axis=1)
        out[component] = jnp.dot(
            t, order, preferred_element_type=F32, precision=lax.Precision.HIGHEST
        )


def local(fi, mi, c1, g1, s1, c2, g2, s2, sharp):
    c1 = jnp.pad(c1.reshape(64, 27), ((0, 0), (0, 101)))
    vec = lambda a: a.reshape(1, 64)
    vmem = pl.BlockSpec(memory_space=pltpu.VMEM)
    tile = lambda n: pltpu.VMEM((n, 8, 128), F32)
    dma = lambda n: pltpu.SemaphoreType.DMA((n,))
    result = pl.pallas_call(
        kernel,
        out_shape=jax.ShapeDtypeStruct((3, 32, 128), F32),
        in_specs=[vmem] * 8 + [pl.BlockSpec(memory_space=pltpu.SMEM)],
        out_specs=vmem,
        scratch_shapes=[
            pltpu.VMEM((4, 2, 8, 128), F32),
            pltpu.VMEM((14, 2, 24, 128), F32),
            pltpu.VMEM((512, 1024), BF16),
            pltpu.VMEM((27 * 32, 128), F32),
            pltpu.VMEM((3456, 256), BF16),
            pltpu.VMEM((216, 384), BF16),
            pltpu.VMEM((4, 4, 192, 128), F32),
            pltpu.VMEM((3, 4, 192, 384), F32),
            pltpu.VMEM((10, 192, 384), F32),
            pltpu.VMEM((16, 384, 384), F32),
            pltpu.VMEM((3, 384, 128), F32),
            pltpu.VMEM((3, 10, 192, 128), BF16),
            pltpu.VMEM((3, 16, 384, 128), BF16),
            pltpu.VMEM((8, 128, 256), F32),
            pltpu.VMEM((14, 320, 256), F32),
            pltpu.VMEM((2, 1024, 128), F32),
            pltpu.VMEM((2, 34 * 160, 128), F32),
            pltpu.VMEM((2, 34 * 160, 128), BF16),
            pltpu.VMEM((34 * 160, 128), BF16),
            pltpu.VMEM((2, 4, 256, 128), BF16),
            pltpu.VMEM((14 * 160, 256), F32),
            pltpu.VMEM((3, 16, 256), F32),
            tile(8), tile(4), tile(4), tile(8), tile(4), tile(4),
            dma(14), dma(14), dma(13), dma(13), dma(13), dma(13),
        ],
        compiler_params=pltpu.CompilerParams(
            collective_id=0, has_side_effects=True, vmem_limit_bytes=60 * 1024 * 1024
        ),
    )(fi, mi, c1, vec(g1), vec(s1), c2, vec(g2), vec(s2), sharp)
    return result.reshape(3, 8, 4, 128)


def solution(mesh):
    placed = (P("depth", "height", None),) * 2 + (P(),) * 7
    return jax.shard_map(
        local,
        mesh=mesh,
        in_specs=placed,
        out_specs=P(None, "depth", "height", None),
        check_vma=False,
    )
```

time: 783 us -> 84.8 us (0.11); the launches traced: 769 us -> 84.5 us
  other arithmetic: 310 us -> 0.76 us
  local copies, waits for them, and re-layouts: 226 us -> 2.15 us
  blocking collectives: 144 us -> 0 us
  Pallas kernels: 0 us -> 81 us
  waiting for transfers between devices: 30.9 us -> 0 us
  starting transfers between devices: 28.5 us -> 0 us
  matrix products: 27 us -> 0 us
    reduce_sum x24 -> x0, other arithmetic: 256 us -> none  [the longest x21 254 us: depth_step(): scores = -factor * jnp.sum(difference * difference, axis=0)]
    slice x11 -> x0, local copies, waits for them, and re-layouts: 178 us -> none  [the longest x7 174 us: depth_step(): depth_plane[:, :, height_shift:height_shift + strip_cells, width_shift:wi...]
    psum x2 -> x0, blocking collectives: 144 us -> none  [the longest x1 72.6 us: local(): lax.psum((jnp.sum(second_raw, axis=(2, 3, 4)), jnp.sum(second_raw * secon...]
    pallas_call x0 -> x1, Pallas kernels: none -> 81 us  [local(): pl.pallas_call(kernel, out_shape=jax.ShapeDtypeStruct((3, 32, 128), F32),...]
    ppermute x12 -> x0, waiting for transfers between devices: 30.9 us -> none  [the longest x6 21.4 us: extended(): after = lax.ppermute(first, axis, down)]
    ppermute x12 -> x0, starting transfers between devices: 28.5 us -> none  [the longest x6 18.5 us: extended(): before = lax.ppermute(last, axis, up)]
    conv_general_dilated x2 -> x0, matrix products: 27 us -> none  [convolve_valid(): lax.conv_general_dilated(field, kernel, (1, 1, 1), 'VALID', dimension_num...]
    add x14 -> x0, other arithmetic: 24.7 us -> none  [the longest x7 18.9 us: depth_step(): running_sum = running_sum * keep + weights]
  transfers between devices with their start and end apart: 12 -> 0, of which waited for: 9 -> 0; matrix products, arithmetic and copies ran while one was open for 1% -> 0% of each run, Pallas kernels for 0% -> 0%
where the time goes in v1:
time: 84.8 us; the launch traced here: 84.5 us
  Pallas kernels  81 us (96%)
  local copies, waits for them, and re-layouts  2.15 us (3%)
    pallas_call x1, Pallas kernels, local(): pl.pallas_call(kernel, out_shape=jax.ShapeDtypeStruct((3, 32, 128), F32),...  81 us

profile of v1, /device:TPU:1, one launch (start us, length us, event | category | flops | bytes accessed | tf_op | source)
XLA Modules:
  0.0 84.5 jit_solution(1252956038403314515)
XLA Ops:
  0.7 0.8 reduce
  1.4 0.1 copy.11
  1.5 0.6 pad.4.c1
  2.1 81.0 %shard_map.91 = f32[3,32,128]{2,1,0:T(8,128)} custom-call(f32[8,4,128]{2,1,0:T(4,128)} %fi.1, f32[8,4,128]{2,1,0:T(4,128)} %mi.1, f32[64,128]{1,0:T(8,128)} %pad.4.c1, f32[1,64]{1,0:T(1,128)} %bitcast.8, f32[1,64]{1,0:T(1,128)} %bitcast.9, bf16[27,4096]{1,0:T(8,128)(2,1)} %c2.1, f32[1,64]{1,0:T(1,128)} %bitcast.10, f32[1,64]{1,0:T(1,128)} %bitcast.11, ...), custom_call_target="tpu_custom_call" | custom-call | tf_op jit(solution)/shard_map/pallas_call | solution.py:512
  83.1 1.4 %copy.15 = f32[3,8,4,128]{3,2,1,0:T(4,128)} copy(f32[3,8,4,128]{3,2,1,0:T(4,128)} %bitcast.7) | data formatting | bytes 98304
  (1 shorter events, 0.0 us)

commit v2 on v1

--- a/solution.py
+++ b/solution.py
@@ -37,15 +37,13 @@
 
 
 def group_peers(depth, height):
-    x_hi, z, y = height // 16, (height // 4) % 4, height % 4
-    along_x, along_y, along_z = [], [], []
+    x_hi, zy = height // 16, height % 16
+    plane = [(depth, x_hi * 16 + (zy + k) % 16) for k in range(1, 16)]
+    along_x = []
     for k in range(1, 8):
         g = (x_hi * 4 + depth + k) % 8
-        along_x.append((g % 4, (g // 4) * 16 + z * 4 + y))
-    for k in range(1, 4):
-        along_y.append((depth, x_hi * 16 + z * 4 + (y + k) % 4))
-        along_z.append((depth, x_hi * 16 + ((z + k) % 4) * 4 + y))
-    return along_x, along_y, along_z
+        along_x.append((g % 4, (g // 4) * 16 + zy))
+    return plane, along_x
 
 
 def halo_peers(depth, height):
@@ -81,29 +79,31 @@
 
 
 def kernel(
-    fi, mi, c1, g1, s1, c2, g2, s2, sharp,
+    fi_h, mi_h, c1_h, g1_h, s1_h, c2_h, g2_h, s2_h, sharp,
     out,
+    fi, mi, c1, g1, s1, c2, g2, s2,
     own, ext, selm, wf, wbig, w1, v, vs, raw1f, raw1m, wmask, xf, xm,
-    raw2f, raw2m, ff, kf, kb, ke, qe, sbuf, res,
-    ax1, ay1, az1, ax2, ay2, az2,
-    hs, hr, as1, ar1, as2, ar2,
+    raw2f, raw2m, ff, kf, kb, ke, qe, sbuf, sbuf2, res,
+    ap1, ax1, ap2, ax2,
+    hs, hr, as1, ar1, as2, ar2, ins,
 ):
     depth, height = position()
     halo = halo_peers(depth, height)
     peers = group_peers(depth, height)
 
     barrier = pltpu.get_barrier_semaphore()
-    everyone = halo + peers[0] + peers[1] + peers[2]
+    everyone = halo + peers[0] + peers[1]
     for peer in everyone:
         pl.semaphore_signal(barrier, inc=1, device_id=peer, device_id_type=MESH)
+    pairs_in = [(fi_h, fi), (mi_h, mi), (c2_h, c2), (c1_h, c1), (g1_h, g1), (s1_h, s1), (g2_h, g2), (s2_h, s2)]
+    loads = [pltpu.make_async_copy(a, b, ins.at[n]) for n, (a, b) in enumerate(pairs_in)]
+    for load in loads:
+        load.start()
+    loads[0].wait()
+    loads[1].wait()
     for h in range(4):
         own[h, 0] = fi[:, h, :]
         own[h, 1] = mi[:, h, :]
-    k_i, n_i = iota((512, 1024), 0), iota((512, 1024), 1)
-    hit = jnp.logical_and(
-        k_i // 128 == (n_i // 32) % 4, k_i % 128 == 4 * (n_i % 32) - 2 + n_i // 128
-    )
-    selm[...] = jnp.where(hit, 1.0, 0.0).astype(BF16)
     pl.semaphore_wait(barrier, len(everyone))
 
     copies = []
@@ -121,7 +121,15 @@
         copy.start()
         copies.append(copy)
 
+    for load in loads[2:]:
+        load.wait()
     ext[5:9, :, 8:16, :] = own[...]
+    n_i = iota((1, 1024), 1)
+    want = 4 * (n_i & 31) - 2 + (n_i >> 7)
+    near = jnp.where(iota((128, 1024), 0) == want, 1.0, 0.0)
+    for hh in range(4):
+        part = jnp.where(((n_i >> 5) & 3) == hh, near, 0.0)
+        selm[hh * 128 : (hh + 1) * 128, :] = part.astype(BF16)
     for pair in range(32):
         wf[pl.ds(pair, 27, stride=32), :] = c2[:, pair * 128 : (pair + 1) * 128].astype(F32)
 
@@ -139,9 +147,10 @@
 
     lax.fori_loop(0, 9, build, 0)
 
-    c1p = jnp.concatenate([c1[pl.ds(0, 32, stride=2), :], c1[pl.ds(1, 32, stride=2), :]], axis=0)
-    c1t = jnp.transpose(c1p)
-    c1t = c1t[:32]
+    r_i, k_i = iota((64, 64), 0), iota((64, 64), 1)
+    even_first = jnp.where(r_i == 2 * (k_i & 31) + (k_i >> 5), 1.0, 0.0)
+    c1t = jnp.concatenate([c1[...].reshape(27, 64), jnp.zeros((5, 64), F32)], axis=0)
+    c1t = jnp.dot(c1t, even_first, preferred_element_type=F32, precision=lax.Precision.HIGHEST)
     zero = jnp.zeros((32, 64), F32)
     spread = jnp.concatenate(
         [jnp.concatenate([c1t if q == u else zero for q in range(6)], axis=1) for u in range(6)],
@@ -170,17 +179,18 @@
         jnp.logical_and(inside, jnp.logical_or(row % 32 < 31, lane < 64)), 1.0, 0.0
     )
     q_i, lane = iota((256, 128), 0), iota((256, 128), 1)
-    w_q = 4 * ((q_i // 32) % 2) + q_i // 64
+    w_q = q_i >> 5
+    e_q = jnp.where(lane - 12 == ((q_i >> 2) & 7), 1.0, 0.0)
+    e_q = jnp.where(jnp.logical_and(lane >= 20, lane - 20 == (q_i & 3)), 1.0, e_q)
+    lane1 = iota((1, 128), 1)
+    in_quad = jnp.logical_and(lane1 >= 24, lane1 < 28)
     for odd in range(2):
         for phase in range(4):
-            w_k = 4 * ((lane - 24 - 2 * odd + 8) % 4 - 1) + phase
-            far = jnp.abs(w_k - w_q) > 3
-            e = jnp.where(jnp.logical_and(lane < 12, lane // 3 == phase), -1.0, 0.0)
-            e = jnp.where(lane - 12 == (q_i // 4) % 8, 1.0, e)
-            e = jnp.where(jnp.logical_and(lane >= 20, lane - 20 == q_i % 4), 1.0, e)
-            in_quad = jnp.logical_and(lane >= 24, lane < 28)
-            e = jnp.where(jnp.logical_and(in_quad, far), -BIG, e)
-            qe[odd, phase] = e.astype(BF16)
+            norm_lane = jnp.logical_and(lane1 < 8, (lane1 >> 1) == phase)
+            w_k = 4 * (((lane1 - 24 - 2 * odd + 8) & 3) - 1) + phase
+            w_k = jnp.where(in_quad, w_k, w_q)
+            e = jnp.where(jnp.abs(w_k - w_q) > 3, -BIG, e_q)
+            qe[odd, phase] = jnp.where(norm_lane, -1.0, e).astype(BF16)
     kf[...] = jnp.zeros_like(kf)
 
     for copy in copies:
@@ -246,7 +256,6 @@
             [
                 jnp.concatenate([sum_f, sum_m], axis=1),
                 jnp.concatenate([sq_f, sq_m], axis=1),
-                jnp.zeros((6, 128), F32),
             ],
             axis=0,
         )
@@ -268,9 +277,12 @@
 
         lax.fori_loop(d0, d1, step, 0)
 
+    def raw_first():
+        raw_fixed()
+        raw_moving(0, 8)
+
     tile = total_over_devices(
-        tile, peers, (ax1, ay1, az1), as1, ar1,
-        (raw_fixed, lambda: raw_moving(0, 8), lambda: raw_moving(8, 16)),
+        tile, peers, (ap1, ax1), as1, ar1, (raw_first, lambda: raw_moving(8, 16)),
     )
 
     def scale_and_offset(tile, gain, shift):
@@ -361,9 +373,12 @@
 
         lax.fori_loop(3, 11, step, 0)
 
+    def both_ends():
+        planes(0, 3)
+        planes(11, 14)
+
     tile = total_over_devices(
-        tile, peers, (ax2, ay2, az2), as2, ar2,
-        (lambda: planes(0, 3), lambda: planes(11, 14), sides),
+        tile, peers, (ap2, ax2), as2, ar2, (both_ends, sides),
     )
     gain2 = jnp.concatenate([g2[...], g2[...]], axis=1)
     shift2 = jnp.concatenate([s2[...], s2[...]], axis=1)
@@ -390,18 +405,16 @@
             scale, offset = pairs2[1][0] * keep, pairs2[1][1] * keep
             for c in range(2):
                 y = raw2m[od, oh * 32 : (oh + 1) * 32, c * 128 : (c + 1) * 128] * scale + offset
-                kf[c, pl.ds(160 + oh * 16 + od, 32, stride=160), :] = rounded(y)
+                kf[c, pl.ds(160 + oh * 16 + od, 32, stride=160), :] = leaky(y)
         return carry
 
     lax.fori_loop(0, 14, spread_moving, 0)
 
     k_i, n_i = iota((512, 128), 0), iota((512, 128), 1)
-    hit = jnp.logical_and(
-        n_i < 12, (k_i // 256) * 2 + (k_i % 128) // 64 == n_i // 3
-    )
+    hit = jnp.logical_and(n_i < 8, (k_i >> 8) * 2 + ((k_i >> 6) & 1) == (n_i >> 1))
     ones = jnp.where(hit, 1.0, 0.0).astype(BF16)
     row, lane = iota((160, 128), 0), iota((160, 128), 1)
-    dd, hh = row % 16 - (lane - 12), row // 16 - (lane - 20)
+    dd, hh = (row & 15) - (lane - 12), (row >> 4) - (lane - 20)
     bad_d = jnp.logical_and(
         jnp.logical_and(lane >= 12, lane < 20), jnp.logical_or(dd < 0, dd > 6)
     )
@@ -409,112 +422,151 @@
         jnp.logical_and(lane >= 20, lane < 24), jnp.logical_or(hh < 0, hh > 6)
     )
     base = jnp.where(jnp.logical_or(bad_d, bad_h), -BIG, 0.0)
-    third = lane % 3
+    base = jnp.concatenate([base, base], axis=0)
+    lane = iota((320, 128), 1)
+    mark = lane - (iota((320, 128), 0) >= 160).astype(I32)
+    odd_lane = (iota((1, 128), 1) & 1) == 1
 
     def keys(q, carry):
-        at = pl.ds(pl.multiple_of(q * 160, 160), 160)
+        at = pl.ds(pl.multiple_of(q * 320, 320), 320)
         squares = []
         for c in range(2):
-            m = kf[c, at, :]
-            kb[c, at, :] = m.astype(BF16)
+            m = kf[c, at, :].astype(BF16)
+            kb[c, at, :] = m
+            m = m.astype(F32)
             sq = m * m
             hi = sq.astype(BF16)
             squares += [hi, (sq - hi.astype(F32)).astype(BF16)]
         norm = dot(jnp.concatenate(squares, axis=1), ones)
         hi = norm.astype(BF16).astype(F32)
-        rest = norm - hi
-        mid = rest.astype(BF16).astype(F32)
-        term = jnp.where(third == 0, hi, jnp.where(third == 1, mid, rest - mid))
-        e = jnp.where(lane == 24 + q % 4, 1.0, base)
-        ke[at, :] = jnp.where(lane < 12, term, e).astype(BF16)
+        term = norm - jnp.where(odd_lane, hi, 0.0)
+        e = jnp.where(mark == 24 + 2 * (q & 1), 1.0, base)
+        ke[at, :] = (term + e).astype(BF16)
         return carry
 
-    lax.fori_loop(0, 34, keys, 0)
+    lax.fori_loop(0, 17, keys, 0)
 
     rate = sharp[0] * (math.log2(math.e) / 64.0)
-    low = iota((64, 128), 1) < 64
-    sub = iota((8, 256), 0).astype(F32)
-    n_i = iota((1, 256), 1)
-    q_w = (4 * ((n_i // 32) % 2) + n_i // 64).astype(F32)
-    q_d = ((n_i // 4) % 8).astype(F32)
-    q_h = (n_i % 4).astype(F32)
-    tiles = [(phase, rel) for phase in range(4) for rel in range(4)
-             if (phase, rel) not in ((0, 0), (3, 3))]
-
-    def block(R, carry):
-        at = pl.ds(pl.multiple_of(R * 64, 64), 64)
-        a, b = 2.0 * ff[0, at, :], 2.0 * ff[1, at, :]
-        ra, rb = pltpu.roll(a, 64, 1), pltpu.roll(b, 64, 1)
-        first = jnp.concatenate([jnp.where(low, t, 0.0) for t in (a, ra, b, rb)], axis=0)
-        second_ = jnp.concatenate([jnp.where(low, 0.0, t) for t in (ra, a, rb, b)], axis=0)
-        query = (first.astype(BF16), second_.astype(BF16))
-        odd = R % 2
-        best = jnp.full((8, 256), -jnp.inf, F32)
-        for phase in range(4):
-            rels = [rel for p, rel in tiles if p == phase]
-            count = len(rels) * 160
-            rows = pl.ds(pl.multiple_of((2 * R + rels[0]) * 160, 160), count)
-            lhs = jnp.concatenate([kb[phase // 2, rows, :], ke[rows, :]], axis=1)
-            rhs = jnp.concatenate([query[phase % 2], qe[odd, phase]], axis=1)
-            score = dot_nt(lhs, rhs)
-            place = tiles.index((phase, rels[0])) * 160
-            sbuf[place : place + count, :] = score
-            best = jnp.maximum(best, jnp.max(score.reshape(count // 8, 8, 256), axis=0))
-        top = jnp.broadcast_to(jnp.max(best, axis=0, keepdims=True), (8, 256))
-        zero = jnp.zeros((8, 256), F32)
-        by_h = [zero] * 10
-        upper, total, w_sum = zero, zero, zero
-        for n, (phase, rel) in enumerate(tiles):
+    low = iota((32, 128), 1) < 64
+    sub = iota((8, 128), 0).astype(F32)
+    n_i = iota((1, 128), 1)
+    q_w = (n_i >> 5).astype(F32)
+    q_d = ((n_i >> 2) & 7).astype(F32)
+    q_h = (n_i & 3).astype(F32)
+    tiles = [
+        [(p, r) for p in range(4) for r in range(4) if -3 <= 4 * (r - 1) + p - 4 * quad <= 6]
+        for quad in range(2)
+    ]
+    zero = jnp.zeros((8, 128), F32)
+
+    def queries(R):
+        first, other = [], []
+        for quad in range(2):
+            at = pl.ds(pl.multiple_of(R * 64 + quad * 32, 32), 32)
+            a, b = 2.0 * ff[0, at, :], 2.0 * ff[1, at, :]
+            ra, rb = pltpu.roll(a, 64, 1), pltpu.roll(b, 64, 1)
+            first += [jnp.where(low, t, 0.0) for t in (a, ra, b, rb)]
+            other += [jnp.where(low, 0.0, t) for t in (ra, a, rb, b)]
+        return [jnp.concatenate(t, axis=0).astype(BF16) for t in (first, other)]
+
+    def scores(R, query, phase, buf, best):
+        rels = [rel for rel in range(4) if any((phase, rel) in t for t in tiles)]
+        count = len(rels) * 160
+        rows = pl.ds(pl.multiple_of((2 * R + rels[0]) * 160, 160), count)
+        lhs = jnp.concatenate([kb[phase // 2, rows, :], ke[rows, :]], axis=1)
+        rhs = jnp.concatenate([query[phase % 2], qe[R & 1, phase]], axis=1)
+        score = dot_nt(lhs, rhs)
+        for n, rel in enumerate(rels):
+            for quad in range(2):
+                if (phase, rel) not in tiles[quad]:
+                    continue
+                place = (quad * 10 + tiles[quad].index((phase, rel))) * 160
+                part = score[n * 160 : n * 160 + 160, quad * 128 : quad * 128 + 128]
+                buf[place : place + 160, :] = part
+                best[quad] = jnp.maximum(best[quad], jnp.max(part.reshape(20, 8, 128), axis=0))
+
+    def weigh(quad, which, buf, top, state):
+        for n in which:
+            phase, rel = tiles[quad][n]
             tile_sum = zero
             for oh in range(10):
-                at_row = n * 160 + oh * 16
-                p0 = jnp.exp2((sbuf[at_row : at_row + 8, :] - top) * rate)
-                p1 = jnp.exp2((sbuf[at_row + 8 : at_row + 16, :] - top) * rate)
+                at_row = (quad * 10 + n) * 160 + oh * 16
+                p0 = jnp.exp2(buf[at_row : at_row + 8, :] * rate - top)
+                p1 = jnp.exp2(buf[at_row + 8 : at_row + 16, :] * rate - top)
                 both = p0 + p1
-                upper = upper + p1
-                by_h[oh] = by_h[oh] + both
+                state["upper"] = state["upper"] + p1
+                state[oh] = state[oh] + both
                 tile_sum = tile_sum + both
-            total = total + tile_sum
-            w_sum = w_sum + tile_sum * float(4 * (rel - 1) + phase)
+            state["total"] = state["total"] + tile_sum
+            state["w"] = state["w"] + tile_sum * float(4 * (rel - 1) + phase - 4 * quad)
+
+    def finish(R, quad, state):
         h_sum = zero
         for oh in range(1, 10):
-            h_sum = h_sum + by_h[oh] * float(oh)
-        d_sum = total * sub + 8.0 * upper
-        weight = jnp.sum(total, axis=0, keepdims=True)
-
-        def mean(s):
-            return jnp.sum(s, axis=0, keepdims=True) / weight
-
-        res[0, pl.ds(R, 1), :] = mean(d_sum) - (q_d + 3.0)
-        res[1, pl.ds(R, 1), :] = mean(h_sum) - (q_h + 3.0)
-        res[2, pl.ds(R, 1), :] = mean(w_sum) - q_w
-        return carry
-
-    lax.fori_loop(0, 16, block, 0)
+            h_sum = h_sum + state[oh] * float(oh)
+        d_sum = state["total"] * sub + 8.0 * state["upper"]
+        weight = jnp.sum(state["total"], axis=0, keepdims=True)
+        for n, (s, own_at) in enumerate(
+            ((d_sum, q_d + 3.0), (h_sum, q_h + 3.0), (state["w"], q_w))
+        ):
+            mean = jnp.sum(s, axis=0, keepdims=True) / weight
+            res[n * 2 + quad, pl.ds(R, 1), :] = mean - own_at
+
+    def step(R, buf, best, R_next, buf_next):
+        query = queries(R_next)
+        best_next = [jnp.full((8, 128), -jnp.inf, F32) for _ in range(2)]
+        for quad in range(2):
+            top = jnp.max(best[quad], axis=0, keepdims=True) * rate
+            top = jnp.broadcast_to(top, (8, 128))
+            state = {k: zero for k in list(range(10)) + ["upper", "total", "w"]}
+            for half in range(2):
+                scores(R_next, query, quad * 2 + half, buf_next, best_next)
+                weigh(quad, range(half * 5, half * 5 + 5), buf, top, state)
+            finish(R, quad, state)
+        return best_next
+
+    def two_blocks(i, best):
+        best = step(2 * i, sbuf, list(best), 2 * i + 1, sbuf2)
+        best = step(2 * i + 1, sbuf2, best, jnp.minimum(2 * i + 2, 15), sbuf)
+        return tuple(best)
+
+    best = [jnp.full((8, 128), -jnp.inf, F32) for _ in range(2)]
+    query = queries(0)
+    for phase in range(4):
+        scores(0, query, phase, sbuf, best)
+    lax.fori_loop(0, 8, two_blocks, tuple(best))
 
     k_i, w_i = iota((128, 128), 0), iota((128, 128), 1)
-    g, blk = k_i // 16, k_i % 16
-    order = jnp.where(w_i == blk * 8 + (g % 2) * 4 + g // 2, 1.0, 0.0)
+    order = jnp.where(w_i == (k_i & 15) * 8 + (k_i >> 4), 1.0, 0.0)
     for component in range(3):
-        t = jnp.transpose(res[component])
-        t = jnp.concatenate([t[n * 32 : (n + 1) * 32] for n in range(8)], axis=1)
+        t = [jnp.transpose(res[component * 2 + quad]) for quad in range(2)]
+        t = [t[n // 4][(n % 4) * 32 : (n % 4) * 32 + 32] for n in range(8)]
+        t = jnp.concatenate(t, axis=1)
         out[component] = jnp.dot(
             t, order, preferred_element_type=F32, precision=lax.Precision.HIGHEST
         )
 
 
 def local(fi, mi, c1, g1, s1, c2, g2, s2, sharp):
-    c1 = jnp.pad(c1.reshape(64, 27), ((0, 0), (0, 101)))
+    c1 = jnp.transpose(c1, (2, 3, 4, 1, 0)).reshape(27, 1, 64)
     vec = lambda a: a.reshape(1, 64)
     vmem = pl.BlockSpec(memory_space=pltpu.VMEM)
-    tile = lambda n: pltpu.VMEM((n, 8, 128), F32)
+    tile = lambda n: pltpu.VMEM((n, 2, 128), F32)
     dma = lambda n: pltpu.SemaphoreType.DMA((n,))
     result = pl.pallas_call(
         kernel,
         out_shape=jax.ShapeDtypeStruct((3, 32, 128), F32),
-        in_specs=[vmem] * 8 + [pl.BlockSpec(memory_space=pltpu.SMEM)],
+        in_specs=[pl.BlockSpec(memory_space=pl.ANY)] * 8 + [pl.BlockSpec(memory_space=pltpu.SMEM)],
         out_specs=vmem,
         scratch_shapes=[
+            pltpu.VMEM((8, 4, 128), F32),
+            pltpu.VMEM((8, 4, 128), F32),
+            pltpu.VMEM((27, 1, 64), F32),
+            pltpu.VMEM((1, 64), F32),
+            pltpu.VMEM((1, 64), F32),
+            pltpu.VMEM((27, 4096), BF16),
+            pltpu.VMEM((1, 64), F32),
+            pltpu.VMEM((1, 64), F32),
             pltpu.VMEM((4, 2, 8, 128), F32),
             pltpu.VMEM((14, 2, 24, 128), F32),
             pltpu.VMEM((512, 1024), BF16),
@@ -535,10 +587,11 @@
             pltpu.VMEM((2, 34 * 160, 128), BF16),
             pltpu.VMEM((34 * 160, 128), BF16),
             pltpu.VMEM((2, 4, 256, 128), BF16),
-            pltpu.VMEM((14 * 160, 256), F32),
-            pltpu.VMEM((3, 16, 256), F32),
-            tile(8), tile(4), tile(4), tile(8), tile(4), tile(4),
-            dma(14), dma(14), dma(13), dma(13), dma(13), dma(13),
+            pltpu.VMEM((20 * 160, 128), F32),
+            pltpu.VMEM((20 * 160, 128), F32),
+            pltpu.VMEM((6, 16, 128), F32),
+            tile(16), tile(8), tile(16), tile(8),
+            dma(14), dma(14), dma(22), dma(22), dma(22), dma(22), dma(8),
         ],
         compiler_params=pltpu.CompilerParams(
             collective_id=0, has_side_effects=True, vmem_limit_bytes=60 * 1024 * 1024

time: 84.8 us -> 72.5 us (0.85)
  Pallas kernels: 81 us -> 70.3 us
    pallas_call x1, Pallas kernels: 81 us -> 70.3 us  [local(): pl.pallas_call(kernel, out_shape=jax.ShapeDtypeStruct((3, 32, 128), F32),...]
where the time goes in v2:
time: 72.5 us; the launch traced here: 72.4 us
  Pallas kernels  70.3 us (97%)
  local copies, waits for them, and re-layouts  1.42 us (2%)
    pallas_call x1, Pallas kernels, local(): pl.pallas_call(kernel, out_shape=jax.ShapeDtypeStruct((3, 32, 128), F32),...  70.3 us

profile of v2, /device:TPU:1, one launch (start us, length us, event | category | flops | bytes accessed | tf_op | source)
XLA Modules:
  0.0 72.4 jit_solution(14796146487408099210)
XLA Ops:
  0.7 70.3 %shard_map.91 = f32[3,32,128]{2,1,0:T(8,128)} custom-call(f32[8,4,128]{2,1,0:T(4,128)} %fi_h.1, f32[8,4,128]{2,1,0:T(4,128)} %mi_h.1, f32[27,1,64]{2,1,0:T(1,128)} %bitcast.9, f32[1,64]{1,0:T(1,128)} %bitcast.10, f32[1,64]{1,0:T(1,128)} %bitcast.11, bf16[27,4096]{1,0:T(8,128)(2,1)} %c2_h.1, f32[1,64]{1,0:T(1,128)} %bitcast.12, f32[1,64]{1,0:T(1,128)} %bitcast.13, ...), custom_call_target="tpu_custom_call" | custom-call | tf_op jit(solution)/shard_map/pallas_call | solution.py:556
  70.9 1.4 %copy.12 = f32[3,8,4,128]{3,2,1,0:T(4,128)} copy(f32[3,8,4,128]{3,2,1,0:T(4,128)} %bitcast.8) | data formatting | bytes 98304

commit v3 on v2

--- a/solution.py
+++ b/solution.py
@@ -82,8 +82,8 @@
     fi_h, mi_h, c1_h, g1_h, s1_h, c2_h, g2_h, s2_h, sharp,
     out,
     fi, mi, c1, g1, s1, c2, g2, s2,
-    own, ext, selm, wf, wbig, w1, v, vs, raw1f, raw1m, wmask, xf, xm,
-    raw2f, raw2m, ff, kf, kb, ke, qe, sbuf, sbuf2, res,
+    own, ext, selm, wf, wbig, w1, v, vs, raw1f, raw1m, xf, xm,
+    ff, kf, kb, ke, qe, sbuf, sbuf2, res,
     ap1, ax1, ap2, ax2,
     hs, hr, as1, ar1, as2, ar2, ins,
 ):
@@ -168,16 +168,6 @@
     w1_hi, w1_lo = dot(pick, spread_hi), dot(pick, spread_lo)
     w1[...] = jnp.concatenate([w1_hi, w1_hi, w1_lo], axis=0).astype(BF16)
 
-    row, lane = iota((384, 128), 0), iota((384, 128), 1)
-    gh = height * 4 - 4 + row // 32
-    inside = jnp.logical_and(gh >= 0, gh < 128)
-    wmask[0] = jnp.where(
-        jnp.logical_and(inside, jnp.logical_or(row % 32 > 0, lane >= 64)), 1.0, 0.0
-    )
-    wmask[1] = jnp.where(inside, 1.0, 0.0)
-    wmask[2] = jnp.where(
-        jnp.logical_and(inside, jnp.logical_or(row % 32 < 31, lane < 64)), 1.0, 0.0
-    )
     q_i, lane = iota((256, 128), 0), iota((256, 128), 1)
     w_q = q_i >> 5
     e_q = jnp.where(lane - 12 == ((q_i >> 2) & 7), 1.0, 0.0)
@@ -199,8 +189,8 @@
     row = iota((48, 128), 0)
     gd = depth * 8 - 8 + row % 24
     d_in = jnp.logical_and(gd >= 0, gd < 32)
-    stacks = []
-    for h4 in range(4):
+
+    def pick_rows(h4):
         parts = []
         for hh in range(4):
             hx = h4 * 4 + hh
@@ -214,18 +204,23 @@
             hi = x.astype(BF16)
             lo = (x - hi.astype(F32)).astype(BF16)
             parts.append(jnp.concatenate([hi, lo], axis=0))
-        stacks.append(jnp.concatenate(parts, axis=1))
-    for h4 in range(4):
-        picked = dot(stacks[h4], selm[...])
+        picked = dot(jnp.concatenate(parts, axis=1), selm[...])
         for q in range(4):
             for j in range(8):
                 v[q, h4, pl.ds(j, 24, stride=8), :] = picked[
                     q * 24 : q * 24 + 24, j * 128 : (j + 1) * 128
                 ]
-    for q in range(4):
-        full = jnp.concatenate([v[q, h4] for h4 in range(4)], axis=1)
-        for b in range(3):
-            vs[b, q] = full[:, 32 * b : 32 * b + 384]
+
+    def shifted(column, rows):
+        for q in range(4):
+            full = jnp.concatenate([v[q, column, rows], v[q, column + 1, rows]], axis=1)
+            for b in range(3):
+                vs[b, q, rows, column * 128 : column * 128 + 128] = full[:, 32 * b : 32 * b + 128]
+
+    own_rows = slice(56, 136)
+    pick_rows(1)
+    pick_rows(2)
+    shifted(1, own_rows)
 
     def patches(image, dx, lane0, lanes):
         start = pl.multiple_of((dx + 3) * 8, 8)
@@ -239,13 +234,14 @@
     def own_sums(dx, sums):
         result = []
         for image in range(2):
-            raw = dot(patches(image, dx, 128, 128), w1[...])
+            lhs = [patches(image, 2 * dx + n, 128, 128) for n in range(2)]
+            raw = dot(jnp.concatenate(lhs, axis=0), w1[...])
             result.append(sums[2 * image] + rows_sum(raw))
             result.append(sums[2 * image + 1] + rows_sum(raw * raw))
         return tuple(result)
 
     start = tuple(jnp.zeros((8, 384), F32) for _ in range(4))
-    sums = lax.fori_loop(4, 12, own_sums, start)
+    sums = lax.fori_loop(2, 6, own_sums, start)
 
     def per_channel(s):
         s = jnp.sum(s, axis=0, keepdims=True)
@@ -278,6 +274,12 @@
         lax.fori_loop(d0, d1, step, 0)
 
     def raw_first():
+        pick_rows(0)
+        pick_rows(3)
+        shifted(1, slice(0, 56))
+        shifted(1, slice(136, 192))
+        shifted(0, slice(0, 192))
+        shifted(2, slice(0, 192))
         raw_fixed()
         raw_moving(0, 8)
 
@@ -309,23 +311,43 @@
         g = depth * 8 + d
         return jnp.where(jnp.logical_and(g >= 0, g < 32), 1.0, 0.0)
 
-    def feat(raw, x, image, dx, out_dx, rows):
-        keep = depth_inside(dx - 4)
-        scale, offset = pairs[image][0] * keep, pairs[image][1] * keep
-        for s in range(3):
-            y = leaky(raw[out_dx, :, s * 128 : (s + 1) * 128] * scale + offset)
-            x[s, out_dx] = (y * wmask[s, rows]).astype(BF16)
-
-    def feat_fixed(dx, carry):
-        feat(raw1f, xf, 0, dx, dx - 3, slice(96, 288))
+    def height_inside(h):
+        g = height * 4 + h
+        return jnp.where(jnp.logical_and(g >= 0, g < 128), 1.0, 0.0)
+
+    row, lane = iota((8, 128), 0), iota((8, 128), 1)
+    not_before = jnp.logical_or(row > 0, lane >= 64)
+    not_after = jnp.logical_or(row < 7, lane < 64)
+
+    def feat(raw, x, image, d, raw_d, x_d, rows, hxs):
+        keep_d = depth_inside(d)
+        for n, hx in enumerate(hxs):
+            keep = keep_d * height_inside(hx - 4)
+            scale, offset = pairs[image][0] * keep, pairs[image][1] * keep
+            at = slice(rows + n * 32, rows + n * 32 + 32)
+            for s in range(3):
+                y = leaky(raw[raw_d, at, s * 128 : (s + 1) * 128] * scale + offset)
+                if s == 0:
+                    y = jnp.concatenate([jnp.where(not_before, y[:8], 0.0), y[8:]], axis=0)
+                if s == 2:
+                    y = jnp.concatenate([y[:24], jnp.where(not_after, y[24:], 0.0)], axis=0)
+                x[s, x_d, at, :] = y.astype(BF16)
+
+    def feat_near(dx, carry):
+        feat(raw1f, xf, 0, dx - 4, dx - 3, dx - 3, 0, range(3, 9))
+        feat(raw1m, xm, 1, dx - 4, dx, dx, 96, range(3, 9))
         return carry
 
-    def feat_moving(dx, carry):
-        feat(raw1m, xm, 1, dx, dx, slice(0, 384))
+    lax.fori_loop(3, 13, feat_near, 0)
+
+    def feat_plane(dx, carry):
+        feat(raw1m, xm, 1, dx - 4, dx, dx, 0, range(12))
         return carry
 
-    lax.fori_loop(3, 13, feat_fixed, 0)
-    lax.fori_loop(0, 16, feat_moving, 0)
+    def feat_sides(dx, carry):
+        feat(raw1m, xm, 1, dx - 4, dx, dx, 0, range(3))
+        feat(raw1m, xm, 1, dx - 4, dx, dx, 288, range(9, 12))
+        return carry
 
     def second(x, od, spans):
         parts = []
@@ -336,11 +358,20 @@
                     parts.append(got[0] if len(got) == 1 else jnp.concatenate(got, axis=0))
         return dot(jnp.concatenate(parts, axis=1), wbig[...])
 
+    def put_keys(raw, od, rows):
+        for n, oh in enumerate(rows):
+            for c in range(2):
+                part = raw[n * 32 : (n + 1) * 32, c * 128 : (c + 1) * 128]
+                kf[c, pl.ds(164 + oh * 16 + od, 32, stride=164), :] = part
+
     def own_second(d, sums):
         raw_f = second(xf, d, ((0, 4),))
-        raw2f[d] = raw_f
+        for h in range(4):
+            for c in range(2):
+                part = raw_f[h * 32 : (h + 1) * 32, c * 128 : (c + 1) * 128]
+                ff[c, pl.ds(d * 4 + h, 32, stride=36), :] = part
         raw_m = second(xm, d + 3, ((3, 4),))
-        raw2m[d + 3, 96:224, :] = raw_m
+        put_keys(raw_m, d + 3, range(3, 7))
         return (
             sums[0] + rows_sum(raw_f),
             sums[1] + rows_sum(raw_f * raw_f),
@@ -359,7 +390,7 @@
 
     def planes(d0, d1):
         def step(od, carry):
-            raw2m[od] = second(xm, od, ((0, 10),))
+            put_keys(second(xm, od, ((0, 10),)), od, range(10))
             return carry
 
         lax.fori_loop(d0, d1, step, 0)
@@ -367,13 +398,15 @@
     def sides():
         def step(od, carry):
             raw = second(xm, od, ((0, 3), (7, 3)))
-            raw2m[od, 0:96, :] = raw[:96]
-            raw2m[od, 224:320, :] = raw[96:]
+            put_keys(raw, od, (0, 1, 2, 7, 8, 9))
             return carry
 
         lax.fori_loop(3, 11, step, 0)
 
     def both_ends():
+        lax.fori_loop(0, 3, feat_plane, 0)
+        lax.fori_loop(13, 16, feat_plane, 0)
+        lax.fori_loop(3, 13, feat_sides, 0)
         planes(0, 3)
         planes(11, 14)
 
@@ -386,29 +419,6 @@
 
     def rounded(y):
         return leaky(y).astype(BF16).astype(F32)
-
-    def spread_fixed(d, carry):
-        scale, offset = pairs2[0]
-        for h in range(4):
-            for c in range(2):
-                y = raw2f[d, h * 32 : (h + 1) * 32, c * 128 : (c + 1) * 128] * scale + offset
-                ff[c, pl.ds(d * 4 + h, 32, stride=32), :] = rounded(y)
-        return carry
-
-    lax.fori_loop(0, 8, spread_fixed, 0)
-
-    def spread_moving(od, carry):
-        keep_d = depth_inside(od - 3)
-        for oh in range(10):
-            gh = height * 4 - 3 + oh
-            keep = jnp.where(jnp.logical_and(gh >= 0, gh < 128), keep_d, 0.0)
-            scale, offset = pairs2[1][0] * keep, pairs2[1][1] * keep
-            for c in range(2):
-                y = raw2m[od, oh * 32 : (oh + 1) * 32, c * 128 : (c + 1) * 128] * scale + offset
-                kf[c, pl.ds(160 + oh * 16 + od, 32, stride=160), :] = leaky(y)
-        return carry
-
-    lax.fori_loop(0, 14, spread_moving, 0)
 
     k_i, n_i = iota((512, 128), 0), iota((512, 128), 1)
     hit = jnp.logical_and(n_i < 8, (k_i >> 8) * 2 + ((k_i >> 6) & 1) == (n_i >> 1))
@@ -425,13 +435,22 @@
     base = jnp.concatenate([base, base], axis=0)
     lane = iota((320, 128), 1)
     mark = lane - (iota((320, 128), 0) >= 160).astype(I32)
+    row = iota((320, 128), 0)
+    row = jnp.where(row >= 160, row - 160, row)
+    gd, gh = depth * 8 - 3 + (row & 15), height * 4 - 3 + (row >> 4)
+    keep = jnp.logical_and(
+        jnp.logical_and(gd >= 0, gd < 32), jnp.logical_and(gh >= 0, gh < 128)
+    )
+    keep = jnp.where(jnp.logical_and(keep, (row & 15) < 14), 1.0, 0.0)
+    scale_m, offset_m = pairs2[1]
     odd_lane = (iota((1, 128), 1) & 1) == 1
 
     def keys(q, carry):
         at = pl.ds(pl.multiple_of(q * 320, 320), 320)
         squares = []
         for c in range(2):
-            m = kf[c, at, :].astype(BF16)
+            m = jnp.concatenate([kf[c, pl.ds(q * 328 + n * 164, 160), :] for n in range(2)], axis=0)
+            m = (leaky(m * scale_m + offset_m) * keep).astype(BF16)
             kb[c, at, :] = m
             m = m.astype(F32)
             sq = m * m
@@ -445,6 +464,10 @@
         return carry
 
     lax.fori_loop(0, 17, keys, 0)
+    for q in (0, 33):
+        at = slice(q * 160, q * 160 + 160)
+        kb[:, at, :] = jnp.zeros((2, 160, 128), BF16)
+        ke[at, :] = jnp.where(lane[:160] == 24 + q % 4, 1.0, base[:160]).astype(BF16)
 
     rate = sharp[0] * (math.log2(math.e) / 64.0)
     low = iota((32, 128), 1) < 64
@@ -462,8 +485,10 @@
     def queries(R):
         first, other = [], []
         for quad in range(2):
-            at = pl.ds(pl.multiple_of(R * 64 + quad * 32, 32), 32)
-            a, b = 2.0 * ff[0, at, :], 2.0 * ff[1, at, :]
+            at = pl.ds(R * 72 + quad * 36, 32)
+            a, b = (
+                2.0 * rounded(ff[c, at, :] * pairs2[0][0] + pairs2[0][1]) for c in range(2)
+            )
             ra, rb = pltpu.roll(a, 64, 1), pltpu.roll(b, 64, 1)
             first += [jnp.where(low, t, 0.0) for t in (a, ra, b, rb)]
             other += [jnp.where(low, 0.0, t) for t in (ra, a, rb, b)]
@@ -577,13 +602,10 @@
             pltpu.VMEM((3, 4, 192, 384), F32),
             pltpu.VMEM((10, 192, 384), F32),
             pltpu.VMEM((16, 384, 384), F32),
-            pltpu.VMEM((3, 384, 128), F32),
             pltpu.VMEM((3, 10, 192, 128), BF16),
             pltpu.VMEM((3, 16, 384, 128), BF16),
-            pltpu.VMEM((8, 128, 256), F32),
-            pltpu.VMEM((14, 320, 256), F32),
-            pltpu.VMEM((2, 1024, 128), F32),
-            pltpu.VMEM((2, 34 * 160, 128), F32),
+            pltpu.VMEM((2, 32 * 36, 128), F32),
+            pltpu.VMEM((2, 34 * 164, 128), F32),
             pltpu.VMEM((2, 34 * 160, 128), BF16),
             pltpu.VMEM((34 * 160, 128), BF16),
             pltpu.VMEM((2, 4, 256, 128), BF16),

time: 72.5 us -> 66 us (0.910)
  Pallas kernels: 70.3 us -> 63.8 us
    pallas_call x1, Pallas kernels: 70.3 us -> 63.8 us  [local(): pl.pallas_call(kernel, out_shape=jax.ShapeDtypeStruct((3, 32, 128), F32),...]
where the time goes in v3:
time: 66 us; the launch traced here: 65.8 us
  Pallas kernels  63.8 us (97%)
  local copies, waits for them, and re-layouts  1.42 us (2%)
  between operations  0.66 us (1%)
    pallas_call x1, Pallas kernels, local(): pl.pallas_call(kernel, out_shape=jax.ShapeDtypeStruct((3, 32, 128), F32),...  63.8 us
    unnamed x1, local copies, waits for them, and re-layouts  1.42 us

profile of v3, /device:TPU:1, one launch (start us, length us, event | category | flops | bytes accessed | tf_op | source)
XLA Modules:
  0.0 65.8 jit_solution(1350580671167984312)
XLA Ops:
  0.7 63.8 %shard_map.91 = f32[3,32,128]{2,1,0:T(8,128)} custom-call(f32[8,4,128]{2,1,0:T(4,128)} %fi_h.1, f32[8,4,128]{2,1,0:T(4,128)} %mi_h.1, f32[27,1,64]{2,1,0:T(1,128)} %bitcast.9, f32[1,64]{1,0:T(1,128)} %bitcast.10, f32[1,64]{1,0:T(1,128)} %bitcast.11, bf16[27,4096]{1,0:T(8,128)(2,1)} %c2_h.1, f32[1,64]{1,0:T(1,128)} %bitcast.12, f32[1,64]{1,0:T(1,128)} %bitcast.13, ...), custom_call_target="tpu_custom_call" | custom-call | tf_op jit(solution)/shard_map/pallas_call | solution.py:581
  64.4 1.4 %copy.12 = f32[3,8,4,128]{3,2,1,0:T(4,128)} copy(f32[3,8,4,128]{3,2,1,0:T(4,128)} %bitcast.8) | data formatting | bytes 98304

commit v4 on v3

--- a/solution.py
+++ b/solution.py
@@ -51,25 +51,21 @@
 
 
 def total_over_devices(value, peers, bufs, send_sems, recv_sems, works):
-    count = 0
-    for group, buf, work in zip(peers, bufs, works):
+    for g, (group, buf, work) in enumerate(zip(peers, bufs, works)):
         buf[0] = value
-        copies = []
         for k, peer in enumerate(group):
-            copy = pltpu.make_async_remote_copy(
+            pltpu.make_async_remote_copy(
                 src_ref=buf.at[0],
                 dst_ref=buf.at[k + 1],
-                send_sem=send_sems.at[count],
-                recv_sem=recv_sems.at[count],
+                send_sem=send_sems.at[g],
+                recv_sem=recv_sems.at[g],
                 device_id=peer,
                 device_id_type=MESH,
-            )
-            copy.start()
-            copies.append(copy)
-            count += 1
+            ).start()
         work()
-        for copy in copies:
-            copy.wait()
+        tiles = buf.at[pl.ds(1, len(group))]
+        pltpu.make_async_copy(tiles, tiles, recv_sems.at[g]).wait()
+        pltpu.make_async_copy(tiles, tiles, send_sems.at[g]).wait()
         value = jnp.sum(buf[...], axis=0)
     return value
 
@@ -91,14 +87,14 @@
     halo = halo_peers(depth, height)
     peers = group_peers(depth, height)
 
+    pairs_in = [(fi_h, fi), (mi_h, mi), (c2_h, c2), (c1_h, c1), (g1_h, g1), (s1_h, s1), (g2_h, g2), (s2_h, s2)]
+    loads = [pltpu.make_async_copy(a, b, ins.at[n]) for n, (a, b) in enumerate(pairs_in)]
+    for load in loads:
+        load.start()
     barrier = pltpu.get_barrier_semaphore()
     everyone = halo + peers[0] + peers[1]
     for peer in everyone:
         pl.semaphore_signal(barrier, inc=1, device_id=peer, device_id_type=MESH)
-    pairs_in = [(fi_h, fi), (mi_h, mi), (c2_h, c2), (c1_h, c1), (g1_h, g1), (s1_h, s1), (g2_h, g2), (s2_h, s2)]
-    loads = [pltpu.make_async_copy(a, b, ins.at[n]) for n, (a, b) in enumerate(pairs_in)]
-    for load in loads:
-        load.start()
     loads[0].wait()
     loads[1].wait()
     for h in range(4):
@@ -110,16 +106,18 @@
     for n, (dd, hh) in enumerate(HALO):
         h0, h1, land = HEIGHT_SPAN[hh]
         block = 8 - 8 * dd
+        which = {1: 0, -1: 1}.get(dd, 2 + (hh + 2 if hh < 0 else hh + 1))
         copy = pltpu.make_async_remote_copy(
             src_ref=own.at[pl.ds(h0, h1 - h0)],
             dst_ref=ext.at[pl.ds(land, h1 - h0), :, pl.ds(block, 8), :],
-            send_sem=hs.at[n],
-            recv_sem=hr.at[n],
+            send_sem=hs.at[which],
+            recv_sem=hr.at[which],
             device_id=halo[n],
             device_id_type=MESH,
         )
         copy.start()
-        copies.append(copy)
+        if dd == 0:
+            copies.append(copy)
 
     for load in loads[2:]:
         load.wait()
@@ -185,6 +183,10 @@
 
     for copy in copies:
         copy.wait()
+    for which, block in ((0, 0), (1, 16)):
+        planes_in = ext.at[:, :, pl.ds(block, 8), :]
+        pltpu.make_async_copy(planes_in, planes_in, hr.at[which]).wait()
+        pltpu.make_async_copy(planes_in, planes_in, hs.at[which]).wait()
 
     row = iota((48, 128), 0)
     gd = depth * 8 - 8 + row % 24
@@ -349,12 +351,12 @@
         feat(raw1m, xm, 1, dx - 4, dx, dx, 288, range(9, 12))
         return carry
 
-    def second(x, od, spans):
+    def second(*spans):
         parts = []
         for a in range(3):
             for b in range(3):
                 for s in range(3):
-                    got = [x[s, od + a, (h + b) * 32 : (h + b + n) * 32, :] for h, n in spans]
+                    got = [x[s, od + a, (h + b) * 32 : (h + b + n) * 32, :] for x, od, h, n in spans]
                     parts.append(got[0] if len(got) == 1 else jnp.concatenate(got, axis=0))
         return dot(jnp.concatenate(parts, axis=1), wbig[...])
 
@@ -364,14 +366,18 @@
                 part = raw[n * 32 : (n + 1) * 32, c * 128 : (c + 1) * 128]
                 kf[c, pl.ds(164 + oh * 16 + od, 32, stride=164), :] = part
 
-    def own_second(d, sums):
-        raw_f = second(xf, d, ((0, 4),))
-        for h in range(4):
-            for c in range(2):
-                part = raw_f[h * 32 : (h + 1) * 32, c * 128 : (c + 1) * 128]
-                ff[c, pl.ds(d * 4 + h, 32, stride=36), :] = part
-        raw_m = second(xm, d + 3, ((3, 4),))
-        put_keys(raw_m, d + 3, range(3, 7))
+    def own_second(d2, sums):
+        spans = [(x, 2 * d2 + n + first, h, 4) for x, first, h in ((xf, 0, 0), (xm, 3, 3)) for n in range(2)]
+        raw = second(*spans)
+        for n in range(2):
+            d = 2 * d2 + n
+            for h in range(4):
+                for c in range(2):
+                    at = n * 128 + h * 32
+                    part = raw[at : at + 32, c * 128 : (c + 1) * 128]
+                    ff[c, pl.ds(d * 4 + h, 32, stride=36), :] = part
+            put_keys(raw[256 + n * 128 : 384 + n * 128], d + 3, range(3, 7))
+        raw_f, raw_m = raw[:256], raw[256:]
         return (
             sums[0] + rows_sum(raw_f),
             sums[1] + rows_sum(raw_f * raw_f),
@@ -380,7 +386,7 @@
         )
 
     start = tuple(jnp.zeros((8, 256), F32) for _ in range(4))
-    sums = lax.fori_loop(0, 8, own_second, start)
+    sums = lax.fori_loop(0, 4, own_second, start)
 
     def per_channel_two(s):
         s = jnp.sum(s, axis=0, keepdims=True)
@@ -390,18 +396,20 @@
 
     def planes(d0, d1):
         def step(od, carry):
-            put_keys(second(xm, od, ((0, 10),)), od, range(10))
+            put_keys(second((xm, od, 0, 10)), od, range(10))
             return carry
 
         lax.fori_loop(d0, d1, step, 0)
 
     def sides():
         def step(od, carry):
-            raw = second(xm, od, ((0, 3), (7, 3)))
-            put_keys(raw, od, (0, 1, 2, 7, 8, 9))
+            first = 3 + 2 * od
+            raw = second(*[(xm, first + n, h, 3) for n in range(2) for h in (0, 7)])
+            for n in range(2):
+                put_keys(raw[n * 192 : n * 192 + 192], first + n, (0, 1, 2, 7, 8, 9))
             return carry
 
-        lax.fori_loop(3, 11, step, 0)
+        lax.fori_loop(0, 4, step, 0)
 
     def both_ends():
         lax.fori_loop(0, 3, feat_plane, 0)
@@ -442,7 +450,7 @@
         jnp.logical_and(gd >= 0, gd < 32), jnp.logical_and(gh >= 0, gh < 128)
     )
     keep = jnp.where(jnp.logical_and(keep, (row & 15) < 14), 1.0, 0.0)
-    scale_m, offset_m = pairs2[1]
+    scale_m, offset_m = pairs2[1][0] * keep, pairs2[1][1] * keep
     odd_lane = (iota((1, 128), 1) & 1) == 1
 
     def keys(q, carry):
@@ -450,8 +458,9 @@
         squares = []
         for c in range(2):
             m = jnp.concatenate([kf[c, pl.ds(q * 328 + n * 164, 160), :] for n in range(2)], axis=0)
-            m = (leaky(m * scale_m + offset_m) * keep).astype(BF16)
-            kb[c, at, :] = m
+            m = leaky(m * scale_m + offset_m).astype(BF16)
+            for n in range(2):
+                kb[c, pl.ds(pl.multiple_of(q * 320 + n * 160, 160), 160), :] = m[n * 160 : n * 160 + 160]
             m = m.astype(F32)
             sq = m * m
             hi = sq.astype(BF16)
@@ -613,7 +622,7 @@
             pltpu.VMEM((20 * 160, 128), F32),
             pltpu.VMEM((6, 16, 128), F32),
             tile(16), tile(8), tile(16), tile(8),
-            dma(14), dma(14), dma(22), dma(22), dma(22), dma(22), dma(8),
+            dma(6), dma(6), dma(2), dma(2), dma(2), dma(2), dma(8),
         ],
         compiler_params=pltpu.CompilerParams(
             collective_id=0, has_side_effects=True, vmem_limit_bytes=60 * 1024 * 1024

time: 66 us -> 63.6 us (0.964)
  Pallas kernels: 63.8 us -> 61.3 us
    pallas_call x1, Pallas kernels: 63.8 us -> 61.3 us  [local(): pl.pallas_call(kernel, out_shape=jax.ShapeDtypeStruct((3, 32, 128), F32),...]
where the time goes in v4:
time: 63.6 us; the launch traced here: 63.4 us
  Pallas kernels  61.3 us (96%)
  local copies, waits for them, and re-layouts  1.42 us (2%)
  between operations  0.66 us (1%)
    pallas_call x1, Pallas kernels, local(): pl.pallas_call(kernel, out_shape=jax.ShapeDtypeStruct((3, 32, 128), F32),...  61.3 us
    unnamed x1, local copies, waits for them, and re-layouts  1.42 us

profile of v4, /device:TPU:1, one launch (start us, length us, event | category | flops | bytes accessed | tf_op | source)
XLA Modules:
  0.0 63.4 jit_solution(947163844744577778)
XLA Ops:
  0.7 61.3 %shard_map.91 = f32[3,32,128]{2,1,0:T(8,128)} custom-call(f32[8,4,128]{2,1,0:T(4,128)} %fi_h.1, f32[8,4,128]{2,1,0:T(4,128)} %mi_h.1, f32[27,1,64]{2,1,0:T(1,128)} %bitcast.9, f32[1,64]{1,0:T(1,128)} %bitcast.10, f32[1,64]{1,0:T(1,128)} %bitcast.11, bf16[27,4096]{1,0:T(8,128)(2,1)} %c2_h.1, f32[1,64]{1,0:T(1,128)} %bitcast.12, f32[1,64]{1,0:T(1,128)} %bitcast.13, ...), custom_call_target="tpu_custom_call" | custom-call | tf_op jit(solution)/shard_map/pallas_call | solution.py:590
  62.0 1.4 %copy.12 = f32[3,8,4,128]{3,2,1,0:T(4,128)} copy(f32[3,8,4,128]{3,2,1,0:T(4,128)} %bitcast.8) | data formatting | bytes 98304

commit v5 on v4

--- a/solution.py
+++ b/solution.py
@@ -79,7 +79,7 @@
     out,
     fi, mi, c1, g1, s1, c2, g2, s2,
     own, ext, selm, wf, wbig, w1, v, vs, raw1f, raw1m, xf, xm,
-    ff, kf, kb, ke, qe, sbuf, sbuf2, res,
+    ff, kf, kb, ke, qe, sbuf, sbuf2, res, ones, kept, window,
     ap1, ax1, ap2, ax2,
     hs, hr, as1, ar1, as2, ar2, ins,
 ):
@@ -179,6 +179,31 @@
             w_k = jnp.where(in_quad, w_k, w_q)
             e = jnp.where(jnp.abs(w_k - w_q) > 3, -BIG, e_q)
             qe[odd, phase] = jnp.where(norm_lane, -1.0, e).astype(BF16)
+    k_i, n_i = iota((512, 128), 0), iota((512, 128), 1)
+    hit = jnp.logical_and(n_i < 8, (k_i >> 8) * 2 + ((k_i >> 6) & 1) == (n_i >> 1))
+    ones[...] = jnp.where(hit, 1.0, 0.0).astype(BF16)
+    row, lane = iota((160, 128), 0), iota((160, 128), 1)
+    dd, hh = (row & 15) - (lane - 12), (row >> 4) - (lane - 20)
+    bad_d = jnp.logical_and(
+        jnp.logical_and(lane >= 12, lane < 20), jnp.logical_or(dd < 0, dd > 6)
+    )
+    bad_h = jnp.logical_and(
+        jnp.logical_and(lane >= 20, lane < 24), jnp.logical_or(hh < 0, hh > 6)
+    )
+    base = jnp.where(jnp.logical_or(bad_d, bad_h), -BIG, 0.0)
+    base = jnp.concatenate([base, base], axis=0)
+    lane = iota((320, 128), 1)
+    mark = lane - (iota((320, 128), 0) >= 160).astype(I32)
+    row = iota((320, 128), 0)
+    row = jnp.where(row >= 160, row - 160, row)
+    gd, gh = depth * 8 - 3 + (row & 15), height * 4 - 3 + (row >> 4)
+    keep = jnp.logical_and(
+        jnp.logical_and(gd >= 0, gd < 32), jnp.logical_and(gh >= 0, gh < 128)
+    )
+    kept[...] = jnp.where(jnp.logical_and(keep, (row & 15) < 14), 1.0, 0.0)
+    for odd in range(2):
+        window[odd] = jnp.where(mark == 24 + 2 * odd, 1.0, base)
+
     kf[...] = jnp.zeros_like(kf)
 
     for copy in copies:
@@ -236,14 +261,14 @@
     def own_sums(dx, sums):
         result = []
         for image in range(2):
-            lhs = [patches(image, 2 * dx + n, 128, 128) for n in range(2)]
+            lhs = [patches(image, 4 * dx + n, 128, 128) for n in range(4)]
             raw = dot(jnp.concatenate(lhs, axis=0), w1[...])
             result.append(sums[2 * image] + rows_sum(raw))
             result.append(sums[2 * image + 1] + rows_sum(raw * raw))
         return tuple(result)
 
     start = tuple(jnp.zeros((8, 384), F32) for _ in range(4))
-    sums = lax.fori_loop(2, 6, own_sums, start)
+    sums = lax.fori_loop(1, 3, own_sums, start)
 
     def per_channel(s):
         s = jnp.sum(s, axis=0, keepdims=True)
@@ -273,7 +298,7 @@
             raw1m[dx] = dot(patches(1, dx, 0, 384), w1[...])
             return carry
 
-        lax.fori_loop(d0, d1, step, 0)
+        lax.fori_loop(d0, d1, step, 0, unroll=2)
 
     def raw_first():
         pick_rows(0)
@@ -428,29 +453,7 @@
     def rounded(y):
         return leaky(y).astype(BF16).astype(F32)
 
-    k_i, n_i = iota((512, 128), 0), iota((512, 128), 1)
-    hit = jnp.logical_and(n_i < 8, (k_i >> 8) * 2 + ((k_i >> 6) & 1) == (n_i >> 1))
-    ones = jnp.where(hit, 1.0, 0.0).astype(BF16)
-    row, lane = iota((160, 128), 0), iota((160, 128), 1)
-    dd, hh = (row & 15) - (lane - 12), (row >> 4) - (lane - 20)
-    bad_d = jnp.logical_and(
-        jnp.logical_and(lane >= 12, lane < 20), jnp.logical_or(dd < 0, dd > 6)
-    )
-    bad_h = jnp.logical_and(
-        jnp.logical_and(lane >= 20, lane < 24), jnp.logical_or(hh < 0, hh > 6)
-    )
-    base = jnp.where(jnp.logical_or(bad_d, bad_h), -BIG, 0.0)
-    base = jnp.concatenate([base, base], axis=0)
-    lane = iota((320, 128), 1)
-    mark = lane - (iota((320, 128), 0) >= 160).astype(I32)
-    row = iota((320, 128), 0)
-    row = jnp.where(row >= 160, row - 160, row)
-    gd, gh = depth * 8 - 3 + (row & 15), height * 4 - 3 + (row >> 4)
-    keep = jnp.logical_and(
-        jnp.logical_and(gd >= 0, gd < 32), jnp.logical_and(gh >= 0, gh < 128)
-    )
-    keep = jnp.where(jnp.logical_and(keep, (row & 15) < 14), 1.0, 0.0)
-    scale_m, offset_m = pairs2[1][0] * keep, pairs2[1][1] * keep
+    scale_m, offset_m = pairs2[1][0] * kept[...], pairs2[1][1] * kept[...]
     odd_lane = (iota((1, 128), 1) & 1) == 1
 
     def keys(q, carry):
@@ -465,18 +468,17 @@
             sq = m * m
             hi = sq.astype(BF16)
             squares += [hi, (sq - hi.astype(F32)).astype(BF16)]
-        norm = dot(jnp.concatenate(squares, axis=1), ones)
+        norm = dot(jnp.concatenate(squares, axis=1), ones[...])
         hi = norm.astype(BF16).astype(F32)
         term = norm - jnp.where(odd_lane, hi, 0.0)
-        e = jnp.where(mark == 24 + 2 * (q & 1), 1.0, base)
-        ke[at, :] = (term + e).astype(BF16)
+        ke[at, :] = (term + window[q & 1]).astype(BF16)
         return carry
 
     lax.fori_loop(0, 17, keys, 0)
     for q in (0, 33):
         at = slice(q * 160, q * 160 + 160)
         kb[:, at, :] = jnp.zeros((2, 160, 128), BF16)
-        ke[at, :] = jnp.where(lane[:160] == 24 + q % 4, 1.0, base[:160]).astype(BF16)
+        ke[at, :] = window[q // 2 % 2, q % 2 * 160 : q % 2 * 160 + 160].astype(BF16)
 
     rate = sharp[0] * (math.log2(math.e) / 64.0)
     low = iota((32, 128), 1) < 64
@@ -621,6 +623,9 @@
             pltpu.VMEM((20 * 160, 128), F32),
             pltpu.VMEM((20 * 160, 128), F32),
             pltpu.VMEM((6, 16, 128), F32),
+            pltpu.VMEM((512, 128), BF16),
+            pltpu.VMEM((320, 128), F32),
+            pltpu.VMEM((2, 320, 128), F32),
             tile(16), tile(8), tile(16), tile(8),
             dma(6), dma(6), dma(2), dma(2), dma(2), dma(2), dma(8),
         ],

time: 63.6 us -> 62.5 us (0.983)
  Pallas kernels: 61.3 us -> 60.2 us
    pallas_call x1, Pallas kernels: 61.3 us -> 60.2 us  [local(): pl.pallas_call(kernel, out_shape=jax.ShapeDtypeStruct((3, 32, 128), F32),...]
where the time goes in v5:
time: 62.5 us; the launch traced here: 62.3 us
  Pallas kernels  60.2 us (96%)
  local copies, waits for them, and re-layouts  1.42 us (2%)
  between operations  0.66 us (1%)
    pallas_call x1, Pallas kernels, local(): pl.pallas_call(kernel, out_shape=jax.ShapeDtypeStruct((3, 32, 128), F32),...  60.2 us
    unnamed x1, local copies, waits for them, and re-layouts  1.42 us

profile of v5, /device:TPU:1, one launch (start us, length us, event | category | flops | bytes accessed | tf_op | source)
XLA Modules:
  0.0 62.3 jit_solution(5859723863247694208)
XLA Ops:
  0.7 60.2 %shard_map.91 = f32[3,32,128]{2,1,0:T(8,128)} custom-call(f32[8,4,128]{2,1,0:T(4,128)} %fi_h.1, f32[8,4,128]{2,1,0:T(4,128)} %mi_h.1, f32[27,1,64]{2,1,0:T(1,128)} %bitcast.9, f32[1,64]{1,0:T(1,128)} %bitcast.10, f32[1,64]{1,0:T(1,128)} %bitcast.11, bf16[27,4096]{1,0:T(8,128)(2,1)} %c2_h.1, f32[1,64]{1,0:T(1,128)} %bitcast.12, f32[1,64]{1,0:T(1,128)} %bitcast.13, ...), custom_call_target="tpu_custom_call" | custom-call | tf_op jit(solution)/shard_map/pallas_call | solution.py:592
  60.9 1.4 %copy.12 = f32[3,8,4,128]{3,2,1,0:T(4,128)} copy(f32[3,8,4,128]{3,2,1,0:T(4,128)} %bitcast.8) | data formatting | bytes 98304

commit v6 on v5

--- a/solution.py
+++ b/solution.py
@@ -291,7 +291,7 @@
             raw1f[dx - 3] = dot(p[96:288], w1[...])
             return carry
 
-        lax.fori_loop(3, 13, step, 0)
+        lax.fori_loop(3, 13, step, 0, unroll=2)
 
     def raw_moving(d0, d1):
         def step(dx, carry):
@@ -365,7 +365,7 @@
         feat(raw1m, xm, 1, dx - 4, dx, dx, 96, range(3, 9))
         return carry
 
-    lax.fori_loop(3, 13, feat_near, 0)
+    lax.fori_loop(3, 13, feat_near, 0, unroll=2)
 
     def feat_plane(dx, carry):
         feat(raw1m, xm, 1, dx - 4, dx, dx, 0, range(12))
@@ -439,7 +439,7 @@
     def both_ends():
         lax.fori_loop(0, 3, feat_plane, 0)
         lax.fori_loop(13, 16, feat_plane, 0)
-        lax.fori_loop(3, 13, feat_sides, 0)
+        lax.fori_loop(3, 13, feat_sides, 0, unroll=2)
         planes(0, 3)
         planes(11, 14)
 

time: 62.5 us -> 62.4 us (level)
  no operation moved by 1% of the time
where the time goes in v6:
time: 62.4 us; the launch traced here: 62.2 us
  Pallas kernels  60.1 us (96%)
  local copies, waits for them, and re-layouts  1.42 us (2%)
  between operations  0.66 us (1%)
    pallas_call x1, Pallas kernels, local(): pl.pallas_call(kernel, out_shape=jax.ShapeDtypeStruct((3, 32, 128), F32),...  60.1 us
    unnamed x1, local copies, waits for them, and re-layouts  1.42 us

profile of v6, /device:TPU:1, one launch (start us, length us, event | category | flops | bytes accessed | tf_op | source)
XLA Modules:
  0.0 62.2 jit_solution(10175571007473248948)
XLA Ops:
  0.7 60.1 %shard_map.91 = f32[3,32,128]{2,1,0:T(8,128)} custom-call(f32[8,4,128]{2,1,0:T(4,128)} %fi_h.1, f32[8,4,128]{2,1,0:T(4,128)} %mi_h.1, f32[27,1,64]{2,1,0:T(1,128)} %bitcast.9, f32[1,64]{1,0:T(1,128)} %bitcast.10, f32[1,64]{1,0:T(1,128)} %bitcast.11, bf16[27,4096]{1,0:T(8,128)(2,1)} %c2_h.1, f32[1,64]{1,0:T(1,128)} %bitcast.12, f32[1,64]{1,0:T(1,128)} %bitcast.13, ...), custom_call_target="tpu_custom_call" | custom-call | tf_op jit(solution)/shard_map/pallas_call | solution.py:592
  60.8 1.4 %copy.12 = f32[3,8,4,128]{3,2,1,0:T(4,128)} copy(f32[3,8,4,128]{3,2,1,0:T(4,128)} %bitcast.8) | data formatting | bytes 98304
